TPU v7x, 32 devices: a whole 2x2x4 slice. The times are simulated.
32 devices in a mesh: leaf: 4 (over y, x), row: 8 (over z, core).
Axes of the slice: x: 2, y: 2, z: 4, core: 2. Of those that a mesh axis runs over, the one named last changes fastest.
Arguments:
- rhs: bfloat16 [6, 4, 512, 256], P(None, 'leaf', 'row'), may hold values from -6 to 6
- diag_inverse: bfloat16 [4, 6, 512, 512], P('leaf'), as said below
- factor: bfloat16 [4, 58, 512, 512], P('leaf', None, 'row'), as said below
- widths: int32 [6, 4], P(None, 'leaf'), may hold values from 64 to 512, as said below
- structure: int32 [4, 58], P('leaf'), may hold values from 0 to 1, as said below
Outputs:
- forward_solution: bfloat16 [6, 4, 512, 256], P(None, 'leaf', 'row')
- adjoint_solution: bfloat16 [6, 4, 512, 256], P(None, 'leaf', 'row')
Inputs may be any that keep to these rules, and one draw needn't show every extreme that they name: `widths`: every draw has a supernode of exactly 512 columns and one of exactly one eighth of 512 columns. `structure`: 1 where the block is present. Each diag_inverse[j, l] is lower triangular with diagonal entries from 0.5 to 1. `factor`: dense blocks of independent entries.
All inputs are finite; a program needn't handle non-finite values.
Results may differ from a plain program's by a relative error of at most 0.017.
Values may be sent and summed in bfloat16 or wider, within the bound.
No kernel may reach another device: no remote copies, remote signals or barrier semaphores. Data moves between devices by JAX's collectives and lax.ppermute only.
A program may use at most 64 MiB of HBM per device.

v0:
```python
import jax
import jax.numpy as jnp
from jax import lax
from jax.experimental import pallas as pl
from jax.experimental.pallas import tpu as pltpu
from jax.sharding import PartitionSpec as P


F32 = jnp.float32
BF16 = jnp.bfloat16
VMEM_LIMIT = 12 * 2**20


def chip_order(count):
    return tuple(sorted(range(1, count + 1), key=lambda k: (-k.bit_length(), k)))


def leaf_order(count):
    return tuple(range(count, 0, -1))


def from_partner(x, axis, mask):
    return lax.ppermute(x, axis, [(i, i ^ mask) for i in range(lax.axis_size(axis))])


def group_size(level_now, leaf_count):
    return min(2**level_now, leaf_count)


def block_offsets(levels, leaf_count):
    offset_table = {}
    cursor = 0
    for source_level in range(levels):
        for target_level in range(source_level + 1, levels):
            offset_table[source_level, target_level] = cursor
            cursor += group_size(target_level, leaf_count)
    return offset_table


def dot(left, right):
    return jnp.dot(left, right, preferred_element_type=F32)


def call(body, outs, scalars, arrays, scratch=(), limit=VMEM_LIMIT, anywhere=False):
    vmem = pl.BlockSpec(memory_space=pltpu.VMEM)
    given = pl.BlockSpec(memory_space=pltpu.HBM) if anywhere else vmem
    return pl.pallas_call(
        body,
        out_shape=[jax.ShapeDtypeStruct(s, d) for s, d in outs],
        in_specs=[pl.BlockSpec(memory_space=pltpu.SMEM)] * len(scalars) + [given] * len(arrays),
        out_specs=[vmem] * len(outs),
        scratch_shapes=list(scratch),
        compiler_params=pltpu.CompilerParams(vmem_limit_bytes=limit),
    )(*scalars, *arrays)


def aligned(index, size):
    return pl.multiple_of(index * size, size)


def assemble(scalars, own, theirs, places, block_rows):
    width = own.shape[2]
    n = len(places)

    def body(s, own_ref, their_ref, *refs):
        outs, sem = refs[:n], refs[n]
        core = s[1]
        copies = []
        for k, (at, count) in enumerate(places):
            for source, who in ((own_ref, core), (their_ref, 1 - core)):
                copies.append(
                    pltpu.make_async_copy(
                        source.at[pl.ds(at, count)],
                        outs[k].at[:, pl.ds(aligned(who, block_rows), block_rows), :],
                        sem.at[len(copies)],
                    )
                )
        for copy in copies:
            copy.start()
        for copy in copies:
            copy.wait()

    outs = [((count, 2 * block_rows, width), BF16) for _, count in places]
    scratch = [pltpu.SemaphoreType.DMA((2 * n,))]
    return call(body, outs, [scalars], [own, theirs], scratch, anywhere=True)


def solve_and_push(scalars, level, parts, inverse, crit, pending, group, at):
    rows, columns = parts[0].shape
    full = inverse.shape[0]
    n_parts, n_pend = len(parts), 0 if pending is None else 1
    n_crit = 0 if crit is None else 1

    def body(s, w, *refs):
        part_refs = refs[:n_parts]
        inv_ref = refs[n_parts]
        crit_ref = refs[n_parts + 1] if n_crit else None
        pend_ref = refs[n_parts + 2] if n_pend else None
        out = n_parts + 1 + n_crit + n_pend
        y_ref = refs[out]
        outs, x_ref = refs[out + 1 : -1], refs[-1]
        chip, low, width = s[0], s[2] & (group - 1), s[3 + level]
        for k in range(n_parts):
            x_ref[pl.ds(aligned(chip ^ k, rows), rows), :] = part_refs[k][...]
        keep = lax.broadcasted_iota(jnp.int32, (full, columns), 0) < width
        x = jnp.where(keep, x_ref[...], jnp.zeros((), BF16))
        y = jnp.where(keep, dot(inv_ref[...], x), 0.0).astype(BF16)
        y_ref[...] = y
        for k in range(len(outs)):
            p = low ^ k
            product = dot(crit_ref[p], y) * w[at + p].astype(F32)
            if n_pend:
                product = product + pend_ref[p]
            outs[k][...] = product.astype(outs[k].dtype)

    outs = [((full, columns), BF16)]
    if n_crit:
        outs.append(((rows, columns), F32))
        outs += [((rows, columns), BF16)] * (group - 1)
    arrays = list(parts) + [inverse] + [crit] * n_crit + [pending] * n_pend
    return call(body, outs, scalars, arrays, [pltpu.VMEM((full, columns), BF16)])


def push_rest(scalars, level, y, inverse, blocks, pendings, starts, block_rows, rows):
    full, columns = y.shape
    n = len(blocks)
    fresh = pendings is None

    def body(s, w, *refs):
        y_ref, inv_ref = refs[:2]
        l_refs = refs[2 : 2 + n]
        p_refs = refs[2 + n : 2 + n + (0 if fresh else n)]
        outs = refs[2 + n + (0 if fresh else n) : -1]
        turned_ref = refs[-1]
        chip, core, width = s[0], s[1], s[3 + level]
        y_now = y_ref[...]
        keep = lax.broadcasted_iota(jnp.int32, (full, columns), 0) < width
        turned_ref[...] = jnp.where(keep, dot(y_now.T, inv_ref[...]).T, 0.0)
        outs[0][...] = turned_ref[pl.ds(aligned(chip, rows), rows), :]
        for slot, who in ((1, core), (2, 1 - core)):
            outs[slot][...] = y_ref[pl.ds(aligned(chip * 2 + who, block_rows), block_rows), :]
        for k in range(n):
            count = blocks[k].shape[0]
            product = dot(l_refs[k][...].reshape(count * rows, full), y_now)
            product = product.reshape(count, rows, columns)
            for p in range(count):
                term = product[p] * w[starts[k] + p].astype(F32)
                if not fresh:
                    term = term + p_refs[k][p]
                outs[3 + k][p] = term

    outs = [((rows, columns), F32), ((block_rows, columns), BF16), ((block_rows, columns), BF16)]
    outs += [((b.shape[0], rows, columns), F32) for b in blocks]
    arrays = [y, inverse] + list(blocks) + ([] if fresh else list(pendings))
    return call(body, outs, scalars, arrays, [pltpu.VMEM((full, columns), F32)])


def pull_level(scalars, level, gathered, crit, inverse, summed, chips, at):
    rows, columns = gathered[0].shape
    full = inverse.shape[0]
    n = len(gathered)
    n_sum = 0 if summed is None else 1

    def body(s, w, *refs):
        g_refs = refs[:n]
        crit_ref, inv_ref = refs[n : n + 2]
        sum_ref = refs[n + 2] if n_sum else None
        outs = refs[n + 2 + n_sum : -2]
        stack_ref, turned_ref = refs[-2:]
        chip, low, width = s[0], s[2] & (n - 1), s[3 + level]
        for k in range(n):
            p = low ^ k
            weighted = g_refs[k][...].astype(F32) * w[at + p].astype(F32)
            stack_ref[pl.ds(aligned(p, rows), rows), :] = weighted.astype(BF16)
        pulled = dot(stack_ref[...].T, crit_ref[...].reshape(n * rows, full))
        if n_sum:
            pulled = pulled + sum_ref[...]
        keep = lax.broadcasted_iota(jnp.int32, (columns, full), 1) < width
        pulled = jnp.where(keep, pulled, 0.0).astype(BF16)
        turned_ref[...] = jnp.where(keep, dot(pulled, inv_ref[...]), 0.0).T
        for k in range(chips):
            rows_out = turned_ref[pl.ds(aligned(chip ^ k, rows), rows), :]
            outs[k][...] = rows_out.astype(outs[k].dtype)

    outs = [((rows, columns), F32)] + [((rows, columns), BF16)] * (chips - 1)
    arrays = list(gathered) + [crit, inverse] + [summed] * n_sum
    scratch = [pltpu.VMEM((n * rows, columns), BF16), pltpu.VMEM((full, columns), F32)]
    return call(body, outs, scalars, arrays, scratch)


def pull_rest(scalars, gathered, blocks, sums, starts):
    rows, columns = gathered[0].shape
    full = blocks[0].shape[2]
    n, m = len(gathered), len(blocks)
    fresh = sums is None

    def body(s, w, *refs):
        g_refs = refs[:n]
        l_refs = refs[n : n + m]
        s_refs = refs[n + m : n + m + (0 if fresh else m)]
        outs, stack_ref = refs[n + m + (0 if fresh else m) : -1], refs[-1]
        low = s[2] & (n - 1)
        for k in range(m):
            for i in range(n):
                p = low ^ i
                weighted = g_refs[i][...].astype(F32) * w[starts[k] + p].astype(F32)
                stack_ref[pl.ds(aligned(p, rows), rows), :] = weighted.astype(BF16)
            term = dot(stack_ref[...].T, l_refs[k][...].reshape(n * rows, full))
            if not fresh:
                term = term + s_refs[k][...]
            outs[k][...] = term

    outs = [((columns, full), F32)] * m
    arrays = list(gathered) + list(blocks) + ([] if fresh else list(sums))
    scratch = [pltpu.VMEM((n * rows, columns), BF16)]
    return call(body, outs, scalars, arrays, scratch)


def shards(rhs, diag_inverse, factor, widths, structure):
    leaf_count = lax.axis_size("leaf")
    chips = lax.axis_size("row") // 2
    leaf = lax.axis_index("leaf")
    row = lax.axis_index("row")
    chip, core = row // 2, row % 2
    levels, block_rows = rhs.shape[0], rhs.shape[2]
    rows = 2 * block_rows
    half = rhs.shape[3] // 2
    first = core == 0
    offsets = block_offsets(levels, leaf_count)

    def in_order(mine, theirs, axis):
        return jnp.where(
            first,
            jnp.concatenate([mine, theirs], axis),
            jnp.concatenate([theirs, mine], axis),
        )

    left_half, right_half = rhs[:, 0, :, :half], rhs[:, 0, :, half:]
    rhs_theirs = from_partner(jnp.where(first, right_half, left_half), "row", 1)
    rhs_pair = in_order(jnp.where(first, left_half, right_half), rhs_theirs, 1)
    places = jnp.stack([chip, core, leaf]).astype(jnp.int32)
    scalars = [jnp.concatenate([places, widths[:, 0]]), structure[0]]

    own_blocks = factor[0]
    their_blocks = from_partner(own_blocks, "row", 1)
    order = [(s, t) for s in range(levels) for t in range(s + 1, levels)]
    spans = [(offsets[pair], group_size(pair[1], leaf_count)) for pair in order]
    block = dict(
        zip(order, assemble(scalars[0], own_blocks, their_blocks, spans, block_rows))
    )

    def exchange(pieces, axis, scale, order):
        taken = {}
        for k in order:
            taken[k] = from_partner(pieces[k - 1], axis, scale * k)
        return [taken[k] for k in sorted(taken)]

    def exchange_chips(pieces):
        return exchange(pieces, "row", 2, chip_order(len(pieces)))

    def exchange_leaves(pieces):
        return exchange(pieces, "leaf", 1, leaf_order(len(pieces)))

    pending = {t: None for t in range(levels)}
    turned, kept, sent = [], [], []
    for l in range(levels):
        if l == 0:
            residual = rhs_pair[l]
        else:
            update = partial_own
            for piece in exchange_leaves(messages):
                update = update + piece.astype(F32)
            residual = (rhs_pair[l].astype(F32) - update).astype(BF16)
        parts = [residual] + exchange_chips([residual] * (chips - 1))
        inverse = diag_inverse[0, l]
        if l + 1 < levels:
            group = group_size(l + 1, leaf_count)
            y, partial_own, *messages = solve_and_push(
                scalars, l, parts, inverse, block[l, l + 1], pending[l + 1], group, offsets[l, l + 1]
            )
        else:
            (y,) = solve_and_push(scalars, l, parts, inverse, None, None, 1, 0)
        later = list(range(l + 2, levels))
        before = None if l == 0 else [pending[t] for t in later]
        starts = [offsets[l, t] for t in later]
        turned_now, keep, send, *after = push_rest(
            scalars, l, y, inverse, [block[l, t] for t in later], before, starts, block_rows, rows
        )
        pending.update(zip(later, after))
        turned.append(turned_now)
        kept.append(keep)
        sent.append(send)
    forward = in_order(jnp.stack(kept), from_partner(jnp.stack(sent), "row", 1), 2)

    sums = {l: None for l in range(levels)}
    adjoint = [None] * levels
    for l in reversed(range(levels)):
        value = turned[l]
        if l + 1 < levels:
            own_term, *messages = pull_level(
                scalars,
                l,
                gathered,
                block[l, l + 1],
                diag_inverse[0, l],
                sums[l],
                chips,
                offsets[l, l + 1],
            )
            total = own_term
            for piece in exchange_chips(messages):
                total = total + piece.astype(F32)
            value = value - total
        now = value.astype(BF16)
        adjoint[l] = now
        if l > 0:
            group = group_size(l, leaf_count)
            gathered = [now] + exchange_leaves([now] * (group - 1))
            sources = list(range(l - 1))
            if sources:
                before = None if l + 1 == levels else [sums[s] for s in sources]
                starts = [offsets[s, l] for s in sources]
                after = pull_rest(scalars, gathered, [block[s, l] for s in sources], before, starts)
                sums.update(zip(sources, after))
    stacked = jnp.stack(adjoint)
    low_rows, high_rows = stacked[:, :block_rows], stacked[:, block_rows:]
    theirs = from_partner(jnp.where(first, high_rows, low_rows), "row", 1)
    backward = in_order(jnp.where(first, low_rows, high_rows), theirs, 2)
    return forward[:, None], backward[:, None]


def solution(mesh):
    placed = (
        P(None, "leaf", "row", None),
        P("leaf", None, None, None),
        P("leaf", None, "row", None),
        P(None, "leaf"),
        P("leaf", None),
    )

    def solve(rhs, diag_inverse, factor, widths, structure):
        step = jax.shard_map(
            shards,
            mesh=mesh,
            in_specs=placed,
            out_specs=(P(None, "leaf", "row", None), P(None, "leaf", "row", None)),
            check_vma=False,
        )
        return step(rhs, diag_inverse, factor, widths, structure)

    return solve
```

profile of v0, /device:TPU:0, one launch (start us, length us, event | category | flops | bytes accessed | tf_op | source)
XLA Modules:
  0.0 181.8 jit_solution(13036300564332468674)
XLA Ops:
  2.3 2.0 %slice_bitcast_fusion = (bf16[512,512]{1,0:T(8,128)(2,1)S(1)}, bf16[512,512]{1,0:T(8,128)(2,1)S(1)}, bf16[512,512]{1,0:T(8,128)(2,1)S(1)}, bf16[512,512]{1,0:T(8...) fusion(bf16[1,6,512,512]{3,2,1,0:T(8,128)(2,1)} %param.6), kind=kLoop, calls=%fused_computation | loop fusion | bytes 6291456 | tf_op jit(solution)/shard_map/squeeze | solution.py:275
  4.3 3.5 %collective-permute-done = bf16[6,64,128]{2,1,0:T(8,128)(2,1)S(1)} collective-permute-done((bf16[6,64,128]{2,1,0:T(8,128)(2,1)S(1)}, bf16[6,64,128]{2,1,0:T(8,128)(2,1)S(1)}, u32[]{:S(2)}, u32[]{:S(2)}) %collective-permute-start) | collective-permute-done | bytes 98336 | tf_op jit(solution)/shard_map/ppermute | solution.py:23
  7.8 3.0 %collective-permute-start.1 = (bf16[128,128]{1,0:T(8,128)(2,1)S(1)}, bf16[128,128]{1,0:T(8,128)(2,1)S(1)}, u32[]{:S(2)}, u32[]{:S(2)}) collective-permute-start(bf16[128,128]{1,0:T(8,128)(2,1)S(1)} %slice_bitcast_fusion.11.refs_0_), channel_id=1, source_target_pairs={{0,2},{1,3},{2,0},{3,1},{4,6},{5,7},{6,4},{7,5},{8,10},{9,11},{10,... | collective-permute-start | bytes 98312 | tf_op jit(solution)/shard_map/ppermute | solution.py:23
  10.8 2.6 %collective-permute-start.2 = (bf16[128,128]{1,0:T(8,128)(2,1)S(1)}, bf16[128,128]{1,0:T(8,128)(2,1)S(1)}, u32[]{:S(2)}, u32[]{:S(2)}) collective-permute-start(bf16[128,128]{1,0:T(8,128)(2,1)S(1)} %slice_bitcast_fusion.11.refs_0_), channel_id=1, source_target_pairs={{0,4},{1,5},{2,6},{3,7},{4,0},{5,1},{6,2},{7,3},{8,12},{9,13},{10,... | collective-permute-start | bytes 98312 | tf_op jit(solution)/shard_map/ppermute | solution.py:23
  13.5 2.1 %copy-done = bf16[1,58,64,512]{3,2,1,0:T(8,128)(2,1)S(1)} copy-done((bf16[1,58,64,512]{3,2,1,0:T(8,128)(2,1)S(1)}, bf16[1,58,64,512]{3,2,1,0:T(8,128)(2,1)}, u32[]{:S(2)}) %copy-start) | copy-done | bytes 3801112
  15.6 3.0 %shard_map.68 = (bf16[2,128,512]{2,1,0:T(8,128)(2,1)S(1)}, bf16[4,128,512]{2,1,0:T(8,128)(2,1)S(1)}, bf16[4,128,512]{2,1,0:T(8,128)(2,1)S(1)}, bf16[4,128,512]{2...) custom-call(s32[9]{0:T(128)S(1)} %pad_add_fusion.s, ...), custom_call_target="tpu_custom_call" | custom-call | tf_op jit(solution)/shard_map/pallas_call | solution.py:47
  21.8 2.4 %collective-permute-done.5 = bf16[128,128]{1,0:T(8,128)(2,1)S(1)} collective-permute-done((bf16[128,128]{1,0:T(8,128)(2,1)S(1)}, bf16[128,128]{1,0:T(8,128)(2,1)S(1)}, u32[]{:S(2)}, u32[]{:S(2)}) %collective-permute-start.5) | collective-permute-done | bytes 32800 | tf_op jit(solution)/shard_map/ppermute | solution.py:23
  24.8 3.5 %collective-permute-start.7 = (bf16[128,128]{1,0:T(8,128)(2,1)S(1)}, bf16[128,128]{1,0:T(8,128)(2,1)S(1)}, u32[]{:S(2)}, u32[]{:S(2)}) collective-permute-start(bf16[128,128]{1,0:T(8,128)(2,1)S(1)} %fusion.6.refs_0_), channel_id=1, source_target_pairs={{0,4},{1,5},{2,6},{3,7},{4,0},{5,1},{6,2},{7,3},{8,12},{9,13},{10,... | collective-permute-start | bytes 98312 | tf_op jit(solution)/shard_map/ppermute | solution.py:23
  30.2 3.8 %collective-permute-done.8.refs_3_ = bf16[128,128]{1,0:T(8,128)(2,1)S(1)} collective-permute-done((bf16[128,128]{1,0:T(8,128)(2,1)S(1)}, bf16[128,128]{1,0:T(8,128)(2,1)S(1)}, u32[]{:S(2)}, u32[]{:S(2)}) %collective-permute-start.8) | collective-permute-done | bytes 32800 | tf_op jit(solution)/shard_map/ppermute | solution.py:23
  35.3 1.6 collective-permute-start.10
  39.3 2.4 %collective-permute-done.11 = bf16[128,128]{1,0:T(8,128)(2,1)S(1)} collective-permute-done((bf16[128,128]{1,0:T(8,128)(2,1)S(1)}, bf16[128,128]{1,0:T(8,128)(2,1)S(1)}, u32[]{:S(2)}, u32[]{:S(2)}) %collective-permute-start.11) | collective-permute-done | bytes 32800 | tf_op jit(solution)/shard_map/ppermute | solution.py:23
  43.4 3.3 %collective-permute-start.14 = (bf16[128,128]{1,0:T(8,128)(2,1)S(1)}, bf16[128,128]{1,0:T(8,128)(2,1)S(1)}, u32[]{:S(2)}, u32[]{:S(2)}) collective-permute-start(bf16[128,128]{1,0:T(8,128)(2,1)S(1)} %fusion.5.refs_0_), channel_id=1, source_target_pairs={{0,6},{1,7},{2,4},{3,5},{4,2},{5,3},{6,0},{7,1},{8,14},{9,15},{10,... | collective-permute-start | bytes 98312 | tf_op jit(solution)/shard_map/ppermute | solution.py:23
  55.4 2.0 %collective-permute-done.17 = bf16[128,128]{1,0:T(8,128)(2,1)S(1)} collective-permute-done((bf16[128,128]{1,0:T(8,128)(2,1)S(1)}, bf16[128,128]{1,0:T(8,128)(2,1)S(1)}, u32[]{:S(2)}, u32[]{:S(2)}) %collective-permute-start.17) | collective-permute-done | bytes 32800 | tf_op jit(solution)/shard_map/ppermute | solution.py:23
  57.6 3.8 %collective-permute-start.19 = (bf16[128,128]{1,0:T(8,128)(2,1)S(1)}, bf16[128,128]{1,0:T(8,128)(2,1)S(1)}, u32[]{:S(2)}, u32[]{:S(2)}) collective-permute-start(bf16[128,128]{1,0:T(8,128)(2,1)S(1)} %fusion.4.refs_0_), channel_id=1, source_target_pairs={{0,4},{1,5},{2,6},{3,7},{4,0},{5,1},{6,2},{7,3},{8,12},{9,13},{10,... | collective-permute-start | bytes 98312 | tf_op jit(solution)/shard_map/ppermute | solution.py:23
  63.3 3.9 %collective-permute-done.20.refs_3_ = bf16[128,128]{1,0:T(8,128)(2,1)S(1)} collective-permute-done((bf16[128,128]{1,0:T(8,128)(2,1)S(1)}, bf16[128,128]{1,0:T(8,128)(2,1)S(1)}, u32[]{:S(2)}, u32[]{:S(2)}) %collective-permute-start.20) | collective-permute-done | bytes 32800 | tf_op jit(solution)/shard_map/ppermute | solution.py:23
  76.5 3.3 %collective-permute-start.26 = (bf16[128,128]{1,0:T(8,128)(2,1)S(1)}, bf16[128,128]{1,0:T(8,128)(2,1)S(1)}, u32[]{:S(2)}, u32[]{:S(2)}) collective-permute-start(bf16[128,128]{1,0:T(8,128)(2,1)S(1)} %fusion.3.refs_0_), channel_id=1, source_target_pairs={{0,6},{1,7},{2,4},{3,5},{4,2},{5,3},{6,0},{7,1},{8,14},{9,15},{10,... | collective-permute-start | bytes 98312 | tf_op jit(solution)/shard_map/ppermute | solution.py:23
  88.5 2.3 %collective-permute-done.29 = bf16[128,128]{1,0:T(8,128)(2,1)S(1)} collective-permute-done((bf16[128,128]{1,0:T(8,128)(2,1)S(1)}, bf16[128,128]{1,0:T(8,128)(2,1)S(1)}, u32[]{:S(2)}, u32[]{:S(2)}) %collective-permute-start.29) | collective-permute-done | bytes 32800 | tf_op jit(solution)/shard_map/ppermute | solution.py:23
  90.9 3.6 %collective-permute-start.31 = (bf16[128,128]{1,0:T(8,128)(2,1)S(1)}, bf16[128,128]{1,0:T(8,128)(2,1)S(1)}, u32[]{:S(2)}, u32[]{:S(2)}) collective-permute-start(bf16[128,128]{1,0:T(8,128)(2,1)S(1)} %fusion.2.refs_0_), channel_id=1, source_target_pairs={{0,4},{1,5},{2,6},{3,7},{4,0},{5,1},{6,2},{7,3},{8,12},{9,13},{10,... | collective-permute-start | bytes 98312 | tf_op jit(solution)/shard_map/ppermute | solution.py:23
  96.7 3.5 %collective-permute-done.32.refs_3_ = bf16[128,128]{1,0:T(8,128)(2,1)S(1)} collective-permute-done((bf16[128,128]{1,0:T(8,128)(2,1)S(1)}, bf16[128,128]{1,0:T(8,128)(2,1)S(1)}, u32[]{:S(2)}, u32[]{:S(2)}) %collective-permute-start.32) | collective-permute-done | bytes 32800 | tf_op jit(solution)/shard_map/ppermute | solution.py:23
  102.0 1.6 collective-permute-start.34
  111.4 3.0 %collective-permute-start.39 = (bf16[128,128]{1,0:T(8,128)(2,1)S(1)}, bf16[128,128]{1,0:T(8,128)(2,1)S(1)}, u32[]{:S(2)}, u32[]{:S(2)}) collective-permute-start(bf16[128,128]{1,0:T(8,128)(2,1)S(1)} %get-tuple-element.166), channel_id=1, source_target_pairs={{0,6},{1,7},{2,4},{3,5},{4,2},{5,3},{6,0},{7,1},{8,14},{9,15},{10,... | collective-permute-start | bytes 98312 | tf_op jit(solution)/shard_map/ppermute | solution.py:23
  115.0 2.2 %collective-permute-done.39 = bf16[128,128]{1,0:T(8,128)(2,1)S(1)} collective-permute-done((bf16[128,128]{1,0:T(8,128)(2,1)S(1)}, bf16[128,128]{1,0:T(8,128)(2,1)S(1)}, u32[]{:S(2)}, u32[]{:S(2)}) %collective-permute-start.39) | collective-permute-done | bytes 32800 | tf_op jit(solution)/shard_map/ppermute | solution.py:23
  122.0 2.1 %collective-permute-done.42.refs_3_ = bf16[128,128]{1,0:T(8,128)(2,1)S(1)} collective-permute-done((bf16[128,128]{1,0:T(8,128)(2,1)S(1)}, bf16[128,128]{1,0:T(8,128)(2,1)S(1)}, u32[]{:S(2)}, u32[]{:S(2)}) %collective-permute-start.42) | collective-permute-done | bytes 32800 | tf_op jit(solution)/shard_map/ppermute | solution.py:23
  125.3 3.6 %collective-permute-start.44 = (bf16[128,128]{1,0:T(8,128)(2,1)S(1)}, bf16[128,128]{1,0:T(8,128)(2,1)S(1)}, u32[]{:S(2)}, u32[]{:S(2)}) collective-permute-start(bf16[128,128]{1,0:T(8,128)(2,1)S(1)} %get-tuple-element.170), channel_id=1, source_target_pairs={{0,4},{1,5},{2,6},{3,7},{4,0},{5,1},{6,2},{7,3},{8,12},{9,13},{10,... | collective-permute-start | bytes 98312 | tf_op jit(solution)/shard_map/ppermute | solution.py:23
  130.8 4.2 %collective-permute-done.45 = bf16[128,128]{1,0:T(8,128)(2,1)S(1)} collective-permute-done((bf16[128,128]{1,0:T(8,128)(2,1)S(1)}, bf16[128,128]{1,0:T(8,128)(2,1)S(1)}, u32[]{:S(2)}, u32[]{:S(2)}) %collective-permute-start.45) | collective-permute-done | bytes 32800 | tf_op jit(solution)/shard_map/ppermute | solution.py:23
  144.3 3.3 %collective-permute-start.51 = (bf16[128,128]{1,0:T(8,128)(2,1)S(1)}, bf16[128,128]{1,0:T(8,128)(2,1)S(1)}, u32[]{:S(2)}, u32[]{:S(2)}) collective-permute-start(bf16[128,128]{1,0:T(8,128)(2,1)S(1)} %get-tuple-element.179), channel_id=1, source_target_pairs={{0,6},{1,7},{2,4},{3,5},{4,2},{5,3},{6,0},{7,1},{8,14},{9,15},{10,... | collective-permute-start | bytes 98312 | tf_op jit(solution)/shard_map/ppermute | solution.py:23
  148.0 2.0 %collective-permute-done.51 = bf16[128,128]{1,0:T(8,128)(2,1)S(1)} collective-permute-done((bf16[128,128]{1,0:T(8,128)(2,1)S(1)}, bf16[128,128]{1,0:T(8,128)(2,1)S(1)}, u32[]{:S(2)}, u32[]{:S(2)}) %collective-permute-start.51) | collective-permute-done | bytes 32800 | tf_op jit(solution)/shard_map/ppermute | solution.py:23
  154.8 2.0 %collective-permute-done.54.refs_3_ = bf16[128,128]{1,0:T(8,128)(2,1)S(1)} collective-permute-done((bf16[128,128]{1,0:T(8,128)(2,1)S(1)}, bf16[128,128]{1,0:T(8,128)(2,1)S(1)}, u32[]{:S(2)}, u32[]{:S(2)}) %collective-permute-start.54) | collective-permute-done | bytes 32800 | tf_op jit(solution)/shard_map/ppermute | solution.py:23
  158.1 3.8 %collective-permute-start.56 = (bf16[128,128]{1,0:T(8,128)(2,1)S(1)}, bf16[128,128]{1,0:T(8,128)(2,1)S(1)}, u32[]{:S(2)}, u32[]{:S(2)}) collective-permute-start(bf16[128,128]{1,0:T(8,128)(2,1)S(1)} %get-tuple-element.185), channel_id=1, source_target_pairs={{0,4},{1,5},{2,6},{3,7},{4,0},{5,1},{6,2},{7,3},{8,12},{9,13},{10,... | collective-permute-start | bytes 98312 | tf_op jit(solution)/shard_map/ppermute | solution.py:23
  163.8 3.8 %collective-permute-done.57 = bf16[128,128]{1,0:T(8,128)(2,1)S(1)} collective-permute-done((bf16[128,128]{1,0:T(8,128)(2,1)S(1)}, bf16[128,128]{1,0:T(8,128)(2,1)S(1)}, u32[]{:S(2)}, u32[]{:S(2)}) %collective-permute-start.57) | collective-permute-done | bytes 32800 | tf_op jit(solution)/shard_map/ppermute | solution.py:23
  173.9 3.3 %collective-permute-start.61 = (bf16[128,128]{1,0:T(8,128)(2,1)S(1)}, bf16[128,128]{1,0:T(8,128)(2,1)S(1)}, u32[]{:S(2)}, u32[]{:S(2)}) collective-permute-start(bf16[128,128]{1,0:T(8,128)(2,1)S(1)} %get-tuple-element.191), channel_id=1, source_target_pairs={{0,6},{1,7},{2,4},{3,5},{4,2},{5,3},{6,0},{7,1},{8,14},{9,15},{10,... | collective-permute-start | bytes 98312 | tf_op jit(solution)/shard_map/ppermute | solution.py:23
  177.7 1.9 %collective-permute-done.61 = bf16[128,128]{1,0:T(8,128)(2,1)S(1)} collective-permute-done((bf16[128,128]{1,0:T(8,128)(2,1)S(1)}, bf16[128,128]{1,0:T(8,128)(2,1)S(1)}, u32[]{:S(2)}, u32[]{:S(2)}) %collective-permute-start.61) | collective-permute-done | bytes 32800 | tf_op jit(solution)/shard_map/ppermute | solution.py:23
  (154 shorter events, 88.1 us)
Async XLA Ops:
  0.6 12.9 %collective-permute-start.4 = (bf16[58,64,512]{2,1,0:T(8,128)(2,1)}, bf16[58,64,512]{2,1,0:T(8,128)(2,1)}, u32[]{:S(2)}, u32[]{:S(2)}) collective-permute-start(bf16[58,64,512]{2,1,0:T(8,128)(2,1)} %bitcast.97), channel_id=1, source_target_pairs={{0,1},{1,0},{2,3},{3,2},{4,5},{5,4},{6,7},{7,6},{8,9},{9,8},{10,11... | collective-permute-start | bytes 11403272 | tf_op jit(solution)/shard_map/ppermute | solution.py:23
  2.2 5.6 %collective-permute-start = (bf16[6,64,128]{2,1,0:T(8,128)(2,1)S(1)}, bf16[6,64,128]{2,1,0:T(8,128)(2,1)S(1)}, u32[]{:S(2)}, u32[]{:S(2)}) collective-permute-start(bf16[6,64,128]{2,1,0:T(8,128)(2,1)S(1)} %get-tuple-element.233), channel_id=1, source_target_pairs={{0,1},{1,0},{2,3},{3,2},{4,5},{5,4},{6,7},{7,6},{8,9},{9,8},{10,11... | collective-permute-start | bytes 294920 | tf_op jit(solution)/shard_map/ppermute | solution.py:23
  7.8 10.8 %collective-permute-start.1 = (bf16[128,128]{1,0:T(8,128)(2,1)S(1)}, bf16[128,128]{1,0:T(8,128)(2,1)S(1)}, u32[]{:S(2)}, u32[]{:S(2)}) collective-permute-start(bf16[128,128]{1,0:T(8,128)(2,1)S(1)} %slice_bitcast_fusion.11.refs_0_), channel_id=1, source_target_pairs={{0,2},{1,3},{2,0},{3,1},{4,6},{5,7},{6,4},{7,5},{8,10},{9,11},{10,... | collective-permute-start | bytes 98312 | tf_op jit(solution)/shard_map/ppermute | solution.py:23
  10.8 7.8 %collective-permute-start.2 = (bf16[128,128]{1,0:T(8,128)(2,1)S(1)}, bf16[128,128]{1,0:T(8,128)(2,1)S(1)}, u32[]{:S(2)}, u32[]{:S(2)}) collective-permute-start(bf16[128,128]{1,0:T(8,128)(2,1)S(1)} %slice_bitcast_fusion.11.refs_0_), channel_id=1, source_target_pairs={{0,4},{1,5},{2,6},{3,7},{4,0},{5,1},{6,2},{7,3},{8,12},{9,13},{10,... | collective-permute-start | bytes 98312 | tf_op jit(solution)/shard_map/ppermute | solution.py:23
  13.4 5.7 %collective-permute-start.3 = (bf16[128,128]{1,0:T(8,128)(2,1)S(1)}, bf16[128,128]{1,0:T(8,128)(2,1)S(1)}, u32[]{:S(2)}, u32[]{:S(2)}) collective-permute-start(bf16[128,128]{1,0:T(8,128)(2,1)S(1)} %slice_bitcast_fusion.11.refs_0_), channel_id=1, source_target_pairs={{0,6},{1,7},{2,4},{3,5},{4,2},{5,3},{6,0},{7,1},{8,14},{9,15},{10,... | collective-permute-start | bytes 98312 | tf_op jit(solution)/shard_map/ppermute | solution.py:23
  24.3 5.8 %collective-permute-start.6 = (bf16[128,128]{1,0:T(8,128)(2,1)S(1)}, bf16[128,128]{1,0:T(8,128)(2,1)S(1)}, u32[]{:S(2)}, u32[]{:S(2)}) collective-permute-start(bf16[128,128]{1,0:T(8,128)(2,1)S(1)} %fusion.6.refs_0_), channel_id=1, source_target_pairs={{0,2},{1,3},{2,0},{3,1},{4,6},{5,7},{6,4},{7,5},{8,10},{9,11},{10,... | collective-permute-start | bytes 98312 | tf_op jit(solution)/shard_map/ppermute | solution.py:23
  24.8 5.4 %collective-permute-start.7 = (bf16[128,128]{1,0:T(8,128)(2,1)S(1)}, bf16[128,128]{1,0:T(8,128)(2,1)S(1)}, u32[]{:S(2)}, u32[]{:S(2)}) collective-permute-start(bf16[128,128]{1,0:T(8,128)(2,1)S(1)} %fusion.6.refs_0_), channel_id=1, source_target_pairs={{0,4},{1,5},{2,6},{3,7},{4,0},{5,1},{6,2},{7,3},{8,12},{9,13},{10,... | collective-permute-start | bytes 98312 | tf_op jit(solution)/shard_map/ppermute | solution.py:23
  28.3 5.7 %collective-permute-start.8 = (bf16[128,128]{1,0:T(8,128)(2,1)S(1)}, bf16[128,128]{1,0:T(8,128)(2,1)S(1)}, u32[]{:S(2)}, u32[]{:S(2)}) collective-permute-start(bf16[128,128]{1,0:T(8,128)(2,1)S(1)} %fusion.6.refs_0_), channel_id=1, source_target_pairs={{0,6},{1,7},{2,4},{3,5},{4,2},{5,3},{6,0},{7,1},{8,14},{9,15},{10,... | collective-permute-start | bytes 98312 | tf_op jit(solution)/shard_map/ppermute | solution.py:23
  42.3 5.7 %collective-permute-start.12 = (bf16[128,128]{1,0:T(8,128)(2,1)S(1)}, bf16[128,128]{1,0:T(8,128)(2,1)S(1)}, u32[]{:S(2)}, u32[]{:S(2)}) collective-permute-start(bf16[128,128]{1,0:T(8,128)(2,1)S(1)} %fusion.5.refs_0_), channel_id=1, source_target_pairs={{0,2},{1,3},{2,0},{3,1},{4,6},{5,7},{6,4},{7,5},{8,10},{9,11},{10,... | collective-permute-start | bytes 98312 | tf_op jit(solution)/shard_map/ppermute | solution.py:23
  42.4 5.6 %collective-permute-start.13 = (bf16[128,128]{1,0:T(8,128)(2,1)S(1)}, bf16[128,128]{1,0:T(8,128)(2,1)S(1)}, u32[]{:S(2)}, u32[]{:S(2)}) collective-permute-start(bf16[128,128]{1,0:T(8,128)(2,1)S(1)} %fusion.5.refs_0_), channel_id=1, source_target_pairs={{0,4},{1,5},{2,6},{3,7},{4,0},{5,1},{6,2},{7,3},{8,12},{9,13},{10,... | collective-permute-start | bytes 98312 | tf_op jit(solution)/shard_map/ppermute | solution.py:23
  43.4 5.7 %collective-permute-start.14 = (bf16[128,128]{1,0:T(8,128)(2,1)S(1)}, bf16[128,128]{1,0:T(8,128)(2,1)S(1)}, u32[]{:S(2)}, u32[]{:S(2)}) collective-permute-start(bf16[128,128]{1,0:T(8,128)(2,1)S(1)} %fusion.5.refs_0_), channel_id=1, source_target_pairs={{0,6},{1,7},{2,4},{3,5},{4,2},{5,3},{6,0},{7,1},{8,14},{9,15},{10,... | collective-permute-start | bytes 98312 | tf_op jit(solution)/shard_map/ppermute | solution.py:23
  52.6 4.8 %collective-permute-start.17 = (bf16[128,128]{1,0:T(8,128)(2,1)S(1)}, bf16[128,128]{1,0:T(8,128)(2,1)S(1)}, u32[]{:S(2)}, u32[]{:S(2)}) collective-permute-start(bf16[128,128]{1,0:T(8,128)(2,1)S(1)} %get-tuple-element.131), channel_id=1, source_target_pairs={{0,24},{8,16},{16,8},{24,0},{1,25},{9,17},{17,9},{25,1},{2,26},{10... | collective-permute-start | bytes 98312 | tf_op jit(solution)/shard_map/ppermute | solution.py:23
  57.4 5.6 %collective-permute-start.18 = (bf16[128,128]{1,0:T(8,128)(2,1)S(1)}, bf16[128,128]{1,0:T(8,128)(2,1)S(1)}, u32[]{:S(2)}, u32[]{:S(2)}) collective-permute-start(bf16[128,128]{1,0:T(8,128)(2,1)S(1)} %fusion.4.refs_0_), channel_id=1, source_target_pairs={{0,2},{1,3},{2,0},{3,1},{4,6},{5,7},{6,4},{7,5},{8,10},{9,11},{10,... | collective-permute-start | bytes 98312 | tf_op jit(solution)/shard_map/ppermute | solution.py:23
  57.6 5.7 %collective-permute-start.19 = (bf16[128,128]{1,0:T(8,128)(2,1)S(1)}, bf16[128,128]{1,0:T(8,128)(2,1)S(1)}, u32[]{:S(2)}, u32[]{:S(2)}) collective-permute-start(bf16[128,128]{1,0:T(8,128)(2,1)S(1)} %fusion.4.refs_0_), channel_id=1, source_target_pairs={{0,4},{1,5},{2,6},{3,7},{4,0},{5,1},{6,2},{7,3},{8,12},{9,13},{10,... | collective-permute-start | bytes 98312 | tf_op jit(solution)/shard_map/ppermute | solution.py:23
  61.4 5.8 %collective-permute-start.20 = (bf16[128,128]{1,0:T(8,128)(2,1)S(1)}, bf16[128,128]{1,0:T(8,128)(2,1)S(1)}, u32[]{:S(2)}, u32[]{:S(2)}) collective-permute-start(bf16[128,128]{1,0:T(8,128)(2,1)S(1)} %fusion.4.refs_0_), channel_id=1, source_target_pairs={{0,6},{1,7},{2,4},{3,5},{4,2},{5,3},{6,0},{7,1},{8,14},{9,15},{10,... | collective-permute-start | bytes 98312 | tf_op jit(solution)/shard_map/ppermute | solution.py:23
  75.4 5.4 %collective-permute-start.24 = (bf16[128,128]{1,0:T(8,128)(2,1)S(1)}, bf16[128,128]{1,0:T(8,128)(2,1)S(1)}, u32[]{:S(2)}, u32[]{:S(2)}) collective-permute-start(bf16[128,128]{1,0:T(8,128)(2,1)S(1)} %fusion.3.refs_0_), channel_id=1, source_target_pairs={{0,2},{1,3},{2,0},{3,1},{4,6},{5,7},{6,4},{7,5},{8,10},{9,11},{10,... | collective-permute-start | bytes 98312 | tf_op jit(solution)/shard_map/ppermute | solution.py:23
  75.5 5.6 %collective-permute-start.25 = (bf16[128,128]{1,0:T(8,128)(2,1)S(1)}, bf16[128,128]{1,0:T(8,128)(2,1)S(1)}, u32[]{:S(2)}, u32[]{:S(2)}) collective-permute-start(bf16[128,128]{1,0:T(8,128)(2,1)S(1)} %fusion.3.refs_0_), channel_id=1, source_target_pairs={{0,4},{1,5},{2,6},{3,7},{4,0},{5,1},{6,2},{7,3},{8,12},{9,13},{10,... | collective-permute-start | bytes 98312 | tf_op jit(solution)/shard_map/ppermute | solution.py:23
  76.5 5.7 %collective-permute-start.26 = (bf16[128,128]{1,0:T(8,128)(2,1)S(1)}, bf16[128,128]{1,0:T(8,128)(2,1)S(1)}, u32[]{:S(2)}, u32[]{:S(2)}) collective-permute-start(bf16[128,128]{1,0:T(8,128)(2,1)S(1)} %fusion.3.refs_0_), channel_id=1, source_target_pairs={{0,6},{1,7},{2,4},{3,5},{4,2},{5,3},{6,0},{7,1},{8,14},{9,15},{10,... | collective-permute-start | bytes 98312 | tf_op jit(solution)/shard_map/ppermute | solution.py:23
  85.7 5.1 %collective-permute-start.29 = (bf16[128,128]{1,0:T(8,128)(2,1)S(1)}, bf16[128,128]{1,0:T(8,128)(2,1)S(1)}, u32[]{:S(2)}, u32[]{:S(2)}) collective-permute-start(bf16[128,128]{1,0:T(8,128)(2,1)S(1)} %get-tuple-element.149), channel_id=1, source_target_pairs={{0,24},{8,16},{16,8},{24,0},{1,25},{9,17},{17,9},{25,1},{2,26},{10... | collective-permute-start | bytes 98312 | tf_op jit(solution)/shard_map/ppermute | solution.py:23
  90.8 5.4 %collective-permute-start.30 = (bf16[128,128]{1,0:T(8,128)(2,1)S(1)}, bf16[128,128]{1,0:T(8,128)(2,1)S(1)}, u32[]{:S(2)}, u32[]{:S(2)}) collective-permute-start(bf16[128,128]{1,0:T(8,128)(2,1)S(1)} %fusion.2.refs_0_), channel_id=1, source_target_pairs={{0,2},{1,3},{2,0},{3,1},{4,6},{5,7},{6,4},{7,5},{8,10},{9,11},{10,... | collective-permute-start | bytes 98312 | tf_op jit(solution)/shard_map/ppermute | solution.py:23
  90.9 5.8 %collective-permute-start.31 = (bf16[128,128]{1,0:T(8,128)(2,1)S(1)}, bf16[128,128]{1,0:T(8,128)(2,1)S(1)}, u32[]{:S(2)}, u32[]{:S(2)}) collective-permute-start(bf16[128,128]{1,0:T(8,128)(2,1)S(1)} %fusion.2.refs_0_), channel_id=1, source_target_pairs={{0,4},{1,5},{2,6},{3,7},{4,0},{5,1},{6,2},{7,3},{8,12},{9,13},{10,... | collective-permute-start | bytes 98312 | tf_op jit(solution)/shard_map/ppermute | solution.py:23
  94.5 5.7 %collective-permute-start.32 = (bf16[128,128]{1,0:T(8,128)(2,1)S(1)}, bf16[128,128]{1,0:T(8,128)(2,1)S(1)}, u32[]{:S(2)}, u32[]{:S(2)}) collective-permute-start(bf16[128,128]{1,0:T(8,128)(2,1)S(1)} %fusion.2.refs_0_), channel_id=1, source_target_pairs={{0,6},{1,7},{2,4},{3,5},{4,2},{5,3},{6,0},{7,1},{8,14},{9,15},{10,... | collective-permute-start | bytes 98312 | tf_op jit(solution)/shard_map/ppermute | solution.py:23
  110.1 4.9 %collective-permute-start.38 = (bf16[128,128]{1,0:T(8,128)(2,1)S(1)}, bf16[128,128]{1,0:T(8,128)(2,1)S(1)}, u32[]{:S(2)}, u32[]{:S(2)}) collective-permute-start(bf16[128,128]{1,0:T(8,128)(2,1)S(1)} %get-tuple-element.165), channel_id=1, source_target_pairs={{0,4},{1,5},{2,6},{3,7},{4,0},{5,1},{6,2},{7,3},{8,12},{9,13},{10,... | collective-permute-start | bytes 98312 | tf_op jit(solution)/shard_map/ppermute | solution.py:23
  111.4 5.7 %collective-permute-start.39 = (bf16[128,128]{1,0:T(8,128)(2,1)S(1)}, bf16[128,128]{1,0:T(8,128)(2,1)S(1)}, u32[]{:S(2)}, u32[]{:S(2)}) collective-permute-start(bf16[128,128]{1,0:T(8,128)(2,1)S(1)} %get-tuple-element.166), channel_id=1, source_target_pairs={{0,6},{1,7},{2,4},{3,5},{4,2},{5,3},{6,0},{7,1},{8,14},{9,15},{10,... | collective-permute-start | bytes 98312 | tf_op jit(solution)/shard_map/ppermute | solution.py:23
  125.3 5.5 %collective-permute-start.44 = (bf16[128,128]{1,0:T(8,128)(2,1)S(1)}, bf16[128,128]{1,0:T(8,128)(2,1)S(1)}, u32[]{:S(2)}, u32[]{:S(2)}) collective-permute-start(bf16[128,128]{1,0:T(8,128)(2,1)S(1)} %get-tuple-element.170), channel_id=1, source_target_pairs={{0,4},{1,5},{2,6},{3,7},{4,0},{5,1},{6,2},{7,3},{8,12},{9,13},{10,... | collective-permute-start | bytes 98312 | tf_op jit(solution)/shard_map/ppermute | solution.py:23
  128.9 6.1 %collective-permute-start.45 = (bf16[128,128]{1,0:T(8,128)(2,1)S(1)}, bf16[128,128]{1,0:T(8,128)(2,1)S(1)}, u32[]{:S(2)}, u32[]{:S(2)}) collective-permute-start(bf16[128,128]{1,0:T(8,128)(2,1)S(1)} %get-tuple-element.171), channel_id=1, source_target_pairs={{0,6},{1,7},{2,4},{3,5},{4,2},{5,3},{6,0},{7,1},{8,14},{9,15},{10,... | collective-permute-start | bytes 98312 | tf_op jit(solution)/shard_map/ppermute | solution.py:23
  143.1 4.9 %collective-permute-start.50 = (bf16[128,128]{1,0:T(8,128)(2,1)S(1)}, bf16[128,128]{1,0:T(8,128)(2,1)S(1)}, u32[]{:S(2)}, u32[]{:S(2)}) collective-permute-start(bf16[128,128]{1,0:T(8,128)(2,1)S(1)} %get-tuple-element.178), channel_id=1, source_target_pairs={{0,4},{1,5},{2,6},{3,7},{4,0},{5,1},{6,2},{7,3},{8,12},{9,13},{10,... | collective-permute-start | bytes 98312 | tf_op jit(solution)/shard_map/ppermute | solution.py:23
  144.3 5.7 %collective-permute-start.51 = (bf16[128,128]{1,0:T(8,128)(2,1)S(1)}, bf16[128,128]{1,0:T(8,128)(2,1)S(1)}, u32[]{:S(2)}, u32[]{:S(2)}) collective-permute-start(bf16[128,128]{1,0:T(8,128)(2,1)S(1)} %get-tuple-element.179), channel_id=1, source_target_pairs={{0,6},{1,7},{2,4},{3,5},{4,2},{5,3},{6,0},{7,1},{8,14},{9,15},{10,... | collective-permute-start | bytes 98312 | tf_op jit(solution)/shard_map/ppermute | solution.py:23
  158.1 5.7 %collective-permute-start.56 = (bf16[128,128]{1,0:T(8,128)(2,1)S(1)}, bf16[128,128]{1,0:T(8,128)(2,1)S(1)}, u32[]{:S(2)}, u32[]{:S(2)}) collective-permute-start(bf16[128,128]{1,0:T(8,128)(2,1)S(1)} %get-tuple-element.185), channel_id=1, source_target_pairs={{0,4},{1,5},{2,6},{3,7},{4,0},{5,1},{6,2},{7,3},{8,12},{9,13},{10,... | collective-permute-start | bytes 98312 | tf_op jit(solution)/shard_map/ppermute | solution.py:23
  162.0 5.7 %collective-permute-start.57 = (bf16[128,128]{1,0:T(8,128)(2,1)S(1)}, bf16[128,128]{1,0:T(8,128)(2,1)S(1)}, u32[]{:S(2)}, u32[]{:S(2)}) collective-permute-start(bf16[128,128]{1,0:T(8,128)(2,1)S(1)} %get-tuple-element.186), channel_id=1, source_target_pairs={{0,6},{1,7},{2,4},{3,5},{4,2},{5,3},{6,0},{7,1},{8,14},{9,15},{10,... | collective-permute-start | bytes 98312 | tf_op jit(solution)/shard_map/ppermute | solution.py:23
  172.8 4.9 %collective-permute-start.60 = (bf16[128,128]{1,0:T(8,128)(2,1)S(1)}, bf16[128,128]{1,0:T(8,128)(2,1)S(1)}, u32[]{:S(2)}, u32[]{:S(2)}) collective-permute-start(bf16[128,128]{1,0:T(8,128)(2,1)S(1)} %get-tuple-element.190), channel_id=1, source_target_pairs={{0,4},{1,5},{2,6},{3,7},{4,0},{5,1},{6,2},{7,3},{8,12},{9,13},{10,... | collective-permute-start | bytes 98312 | tf_op jit(solution)/shard_map/ppermute | solution.py:23
  173.9 5.7 %collective-permute-start.61 = (bf16[128,128]{1,0:T(8,128)(2,1)S(1)}, bf16[128,128]{1,0:T(8,128)(2,1)S(1)}, u32[]{:S(2)}, u32[]{:S(2)}) collective-permute-start(bf16[128,128]{1,0:T(8,128)(2,1)S(1)} %get-tuple-element.191), channel_id=1, source_target_pairs={{0,6},{1,7},{2,4},{3,5},{4,2},{5,3},{6,0},{7,1},{8,14},{9,15},{10,... | collective-permute-start | bytes 98312 | tf_op jit(solution)/shard_map/ppermute | solution.py:23
  (34 other events, 146.5 us)
where the time goes:
time: 182 us
  starting transfers between devices  82.3 us (45%)
  waiting for transfers between devices  65.2 us (36%)
  Pallas kernels  22.3 us (12%)
  local copies, waits for them, and re-layouts  8.06 us (4%)
  other arithmetic  2.86 us (2%)
    ppermute x63, starting transfers between devices, from_partner(): lax.ppermute(x, axis, [(i, i ^ mask) for i in range(lax.axis_size(axis))])  82.3 us
    ppermute x63, waiting for transfers between devices, from_partner(): lax.ppermute(x, axis, [(i, i ^ mask) for i in range(lax.axis_size(axis))])  65.2 us
    pallas_call x18, Pallas kernels, call(): pl.pallas_call(body, out_shape=[jax.ShapeDtypeStruct(s, d) for s, d in ou...  22.3 us
    pallas_call x4, local copies, waits for them, and re-layouts, call(): pl.pallas_call(body, out_shape=[jax.ShapeDtypeStruct(s, d) for s, d in ou...  3.84 us
  transfers between devices with their start and end apart: 63, of which 45 were waited for; matrix products, arithmetic and copies ran while one was open for 4% of the time, Pallas kernels for 5%

commit v1 on v0

v1 whole, which is shorter than its diff:
```python
import jax
import jax.numpy as jnp
from jax import lax
from jax.experimental import pallas as pl
from jax.experimental.pallas import tpu as pltpu
from jax.sharding import PartitionSpec as P


F32 = jnp.float32
BF16 = jnp.bfloat16
VMEM_LIMIT = 16 * 2**20
SKIP_LEVEL = 4


def chip_order(count):
    return tuple(sorted(range(1, count + 1), key=lambda k: (-k.bit_length(), k)))


def leaf_order(count):
    return tuple(range(count, 0, -1))


def from_partner(x, axis, mask):
    return lax.ppermute(x, axis, [(i, i ^ mask) for i in range(lax.axis_size(axis))])


def group_size(level_now, leaf_count):
    return min(2**level_now, leaf_count)


def block_offsets(levels, leaf_count):
    offset_table = {}
    cursor = 0
    for source_level in range(levels):
        for target_level in range(source_level + 1, levels):
            offset_table[source_level, target_level] = cursor
            cursor += group_size(target_level, leaf_count)
    return offset_table


def dot(left, right):
    return jnp.dot(left, right, preferred_element_type=F32)


def call(body, outs, scalars, arrays, scratch=(), far=0):
    vmem = pl.BlockSpec(memory_space=pltpu.VMEM)
    given = [pl.BlockSpec(memory_space=pltpu.HBM)] * far + [vmem] * (len(arrays) - far)
    return pl.pallas_call(
        body,
        out_shape=[jax.ShapeDtypeStruct(s, d) for s, d in outs],
        in_specs=[pl.BlockSpec(memory_space=pltpu.SMEM)] * len(scalars) + given,
        out_specs=[vmem] * len(outs),
        scratch_shapes=list(scratch),
        compiler_params=pltpu.CompilerParams(vmem_limit_bytes=VMEM_LIMIT),
    )(*scalars, *arrays)


def aligned(index, size):
    return pl.multiple_of(index * size, size)


def masked_inverse(inverse, width):
    full = inverse.shape[0]
    down = lax.broadcasted_iota(jnp.int32, (full, full), 0) < width
    along = lax.broadcasted_iota(jnp.int32, (full, full), 1) < width
    return jnp.where(down & along, inverse, jnp.zeros((), BF16))


def fold_blocks(scalars, factor, inverses, spans, picked, blocks, levels, keep):
    _, half, full = factor.shape
    total = sum(count for _, _, count in spans)
    n_out = 1 + len(picked)

    def body(s, w, factor_ref, inverses_ref, *refs):
        out_ref, picked_refs = refs[0], refs[1:n_out]
        own_ref, inv_ref, folded_ref, sem = refs[n_out:]
        used = sorted({level for level, _, _ in spans})
        order = used + [level for level in range(levels) if level not in used]
        copies = [pltpu.make_async_copy(factor_ref.at[pl.ds(0, blocks)], own_ref, sem.at[levels])]
        copies += [
            pltpu.make_async_copy(inverses_ref.at[level], inv_ref.at[level], sem.at[level])
            for level in order
        ]
        for copy in copies:
            copy.start()
        copies.pop(0).wait()
        cursor, last = 0, None
        for i, (level, at, count) in enumerate(spans):
            if level != last:
                copies.pop(0).wait()
                folded_ref[used.index(level)] = masked_inverse(inv_ref[level], s[3 + level])
                last = level
            flat = own_ref[pl.ds(at, count)].reshape(count * half, full)
            product = dot(flat, folded_ref[used.index(level)]).reshape(count, half, full)
            for p in range(count):
                block = (product[p] * w[at + p].astype(F32)).astype(BF16)
                out_ref[cursor + p] = block
                if i in picked:
                    picked_refs[picked.index(i)][p] = block
            cursor += count
        for copy in copies:
            copy.wait()

    outs = [((total, half, full), BF16)]
    outs += [((spans[i][2], half, full), BF16) for i in picked]
    held = [((blocks, half, full), BF16), ((levels, full, full), BF16)]
    scratch = [] if keep else [pltpu.VMEM(*h) for h in held]
    n_used = len({level for level, _, _ in spans})
    scratch += [pltpu.VMEM((n_used, full, full), BF16), pltpu.SemaphoreType.DMA((levels + 1,))]
    arrays = [pltpu.with_memory_space_constraint(x, pltpu.HBM) for x in (factor, inverses)]
    return call(body, outs + (held if keep else []), scalars, arrays, scratch, far=2)


def skip_level(scalars, upper, lower_mine, lower_theirs, folded, at):
    count, half, full = upper[0].shape
    n, chips = len(upper), len(lower_mine)

    def body(s, *refs):
        upper_refs, mine = refs[:n], refs[n : n + chips]
        theirs, folded_ref, out_ref, lower_ref = refs[n + chips :]
        chip, core, leaf = s[0], s[1], s[2]
        total = jnp.zeros((count * half, full), F32)
        for k in range(n):
            p = (leaf ^ k) & (n - 1)
            for q in range(chips):
                place = (chip ^ q) * 2
                lower_ref[k, pl.ds(aligned(place + core, half), half), :] = mine[q][p]
                lower_ref[k, pl.ds(aligned(place + 1 - core, half), half), :] = theirs[q, p]
            total = total + dot(upper_refs[k][...].reshape(count * half, full), lower_ref[k])
        direct = folded_ref[pl.ds(at, count)].astype(F32)
        out_ref[...] = (direct - total.reshape(count, half, full)).astype(BF16)

    outs = [((count, half, full), BF16)]
    arrays = [*upper, *lower_mine, lower_theirs, folded]
    return call(body, outs, scalars[:1], arrays, [pltpu.VMEM((n, full, full), BF16)])


def push(scalars, parts, full, group, pending, pair, at):
    rows, columns = parts[0].shape
    half = rows // 2
    n_parts = len(parts)
    n_pend = 0 if pending is None else 1

    def body(s, *refs):
        part_refs, m_refs = refs[:n_parts], refs[n_parts : n_parts + 2]
        pend_ref = refs[n_parts + 2] if n_pend else None
        outs, x_ref, all_ref = refs[n_parts + 2 + n_pend : -2], *refs[-2:]
        chip, core, leaf = s[0], s[1], s[2]
        for k in range(n_parts):
            x_ref[pl.ds(aligned(chip ^ k, rows), rows), :] = part_refs[k][...]
        for side in range(2):
            flat = m_refs[side][pl.ds(at, group)].reshape(group * half, full)
            all_ref[side] = dot(flat, x_ref[...]).reshape(group, half, columns)
        for k in range(group):
            p = (leaf ^ k) & (group - 1)
            for side, who in enumerate((core, 1 - core)):
                place = pl.ds(aligned(who, half), half)
                total = all_ref[side, p]
                if n_pend:
                    total = total + pend_ref[p, place, :]
                outs[k][place, :] = total.astype(outs[k].dtype)

    outs = [((rows, columns), BF16 if k else F32) for k in range(group)]
    arrays = [*parts, *pair, *([pending] if n_pend else [])]
    scratch = [
        pltpu.VMEM((full, columns), BF16),
        pltpu.VMEM((2, group, half, columns), F32),
    ]
    return call(body, outs, scalars[:1], arrays, scratch)


def finish(scalars, level, parts, inverses, sides, spans, pendings):
    rows, columns = parts[0].shape
    full = inverses.shape[1]
    half = rows // 2
    n, n_parts = len(spans), len(parts)
    n_s = 2 if n else 0
    fresh = pendings is None

    def body(s, w, *refs):
        part_refs, inv_ref = refs[:n_parts], refs[n_parts]
        refs = refs[n_parts + 1 :]
        side_refs, p_refs = refs[:n_s], refs[n_s : n_s + (0 if fresh else n)]
        outs, x_ref, turned_ref, y_ref = refs[n_s + (0 if fresh else n) : -3], *refs[-3:]
        chip, core, width = s[0], s[1], s[3 + level]
        for k in range(n_parts):
            x_ref[pl.ds(aligned(chip ^ k, rows), rows), :] = part_refs[k][...]
        keep = lax.broadcasted_iota(jnp.int32, (full, columns), 0) < width
        x = jnp.where(keep, x_ref[...], jnp.zeros((), BF16))
        y = jnp.where(keep, dot(inv_ref[level], x), 0.0).astype(BF16)
        y_ref[...] = y
        turned_ref[...] = jnp.where(keep, dot(y.T, inv_ref[level]).T, 0.0)
        outs[0][...] = turned_ref[pl.ds(aligned(chip, rows), rows), :]
        for at, who in ((1, core), (2, 1 - core)):
            outs[at][...] = y_ref[pl.ds(aligned(chip * 2 + who, half), half), :]
        for k, (at, count) in enumerate(spans):
            for side, who in enumerate((core, 1 - core)):
                place = pl.ds(aligned(who, half), half)
                product = dot(side_refs[side][pl.ds(at, count)].reshape(count * half, full), y)
                product = product.reshape(count, half, columns)
                for p in range(count):
                    term = product[p] * w[at + p].astype(F32)
                    if not fresh:
                        term = term + p_refs[k][p, place, :]
                    outs[3 + k][p, place, :] = term

    outs = [((rows, columns), F32), ((half, columns), BF16), ((half, columns), BF16)]
    outs += [((count, rows, columns), F32) for _, count in spans]
    arrays = [*parts, inverses, *(sides if n else []), *([] if fresh else pendings)]
    scratch = [
        pltpu.VMEM((full, columns), BF16),
        pltpu.VMEM((full, columns), F32),
        pltpu.VMEM((full, columns), BF16),
    ]
    return call(body, outs, scalars, arrays, scratch)


def two_sides(stack_ref, piece_refs, vector, leaf, core, weights=None):
    count = len(vector)
    half = piece_refs[0].shape[1] // 2
    for k, (array, slot) in enumerate(vector):
        p = (leaf ^ k) & (count - 1)
        for side, who in enumerate((core, 1 - core)):
            piece = piece_refs[array][slot, pl.ds(aligned(who, half), half), :]
            if weights is not None:
                w, start = weights
                piece = (piece.astype(F32) * w[start + p].astype(F32)).astype(BF16)
            stack_ref[side, pl.ds(aligned(p, half), half), :] = piece
    return [stack_ref[side, : count * half, :].T for side in range(2)]


def pull(scalars, pieces, vectors, outputs, pairs, full, chips):
    _, rows, columns = pieces[0].shape
    half = rows // 2
    n_p, n_m = len(pieces), 2 * len(pairs)
    sums = [total for _, total in outputs if total is not None]
    tall = max(len(v) for v in vectors) * half

    def body(s, *refs):
        piece_refs, m_refs = refs[:n_p], refs[n_p : n_p + n_m]
        waiting = list(refs[n_p + n_m : n_p + n_m + len(sums)])
        outs, stack_ref, turned_ref = refs[n_p + n_m + len(sums) : -2], *refs[-2:]
        chip, core, leaf = s[0], s[1], s[2]
        lefts = [
            two_sides(stack_ref.at[i], piece_refs, v, leaf, core) for i, v in enumerate(vectors)
        ]
        for slot, (terms, total) in enumerate(outputs):
            now = None if total is None else waiting.pop(0)[...]
            for v, which, at in terms:
                count = len(vectors[v])
                for side in range(2):
                    flat = m_refs[2 * which + side][pl.ds(at, count)].reshape(count * half, full)
                    product = dot(lefts[v][side], flat)
                    now = product if now is None else now + product
            turned_ref[slot] = now.T
            for k in range(chips):
                block = turned_ref[slot, pl.ds(aligned(chip ^ k, rows), rows), :]
                outs[k][slot] = block.astype(outs[k].dtype)

    outs = [((len(outputs), rows, columns), BF16 if k else F32) for k in range(chips)]
    arrays = [*pieces, *[m for pair in pairs for m in pair], *sums]
    scratch = [
        pltpu.VMEM((len(vectors), 2, tall, columns), BF16),
        pltpu.VMEM((len(outputs), full, columns), F32),
    ]
    return call(body, outs, scalars[:1], arrays, scratch)


def pull_rest(scalars, pieces, vectors, outputs, sides, inverses):
    _, rows, columns = pieces[0].shape
    half = rows // 2
    full = inverses.shape[1]
    n_p = len(pieces)
    sums = [o[2] for o in outputs if o[2] is not None]
    tall = max(len(v) for v in vectors) * half

    def body(s, w, *refs):
        piece_refs, side_refs, inv_ref = refs[:n_p], refs[n_p : n_p + 2], refs[n_p + 2]
        waiting = list(refs[n_p + 3 : n_p + 3 + len(sums)])
        outs, stack_ref = refs[n_p + 3 + len(sums) : -1], refs[-1]
        core, leaf = s[1], s[2]
        for slot, (level, terms, total, complete) in enumerate(outputs):
            now = None if total is None else waiting.pop(0)[...]
            for v, at in terms:
                count = len(vectors[v])
                lefts = two_sides(
                    stack_ref.at[slot], piece_refs, vectors[v], leaf, core, (w, at)
                )
                for side in range(2):
                    flat = side_refs[side][pl.ds(at, count)].reshape(count * half, full)
                    product = dot(lefts[side], flat)
                    now = product if now is None else now + product
            if complete:
                keep = lax.broadcasted_iota(jnp.int32, (columns, full), 1) < s[3 + level]
                now = jnp.where(keep, now, 0.0).astype(BF16)
                now = jnp.where(keep, dot(now, inv_ref[level]), 0.0)
            outs[slot][...] = now

    outs = [((columns, full), F32)] * len(outputs)
    arrays = [*pieces, *sides, inverses, *sums]
    return call(body, outs, scalars, arrays, [pltpu.VMEM((len(outputs), 2, tall, columns), BF16)])


def shards(rhs, diag_inverse, factor, widths, structure):
    leaf_count = lax.axis_size("leaf")
    chips = lax.axis_size("row") // 2
    leaf = lax.axis_index("leaf")
    row = lax.axis_index("row")
    chip, core = row // 2, row % 2
    levels, block_rows = rhs.shape[0], rhs.shape[2]
    half, full = rhs.shape[3] // 2, factor.shape[3]
    first = core == 0
    offsets = block_offsets(levels, leaf_count)
    group = [group_size(l, leaf_count) for l in range(levels)]
    top = levels - 1

    def in_order(mine, theirs, axis):
        return jnp.where(
            first,
            jnp.concatenate([mine, theirs], axis),
            jnp.concatenate([theirs, mine], axis),
        )

    def exchange(pieces, axis, scale, order):
        taken = {}
        for k in order:
            taken[k] = from_partner(pieces[k - 1], axis, scale * k)
        return [taken[k] for k in sorted(taken)]

    def exchange_chips(pieces):
        return exchange(pieces, "row", 2, chip_order(len(pieces)))

    def exchange_leaves(pieces):
        return exchange(pieces, "leaf", 1, leaf_order(len(pieces)))

    def gather_chips(stacked):
        return [stacked] + exchange_chips([stacked] * (chips - 1))

    left_half, right_half = rhs[:, 0, :, :half], rhs[:, 0, :, half:]
    rhs_theirs = from_partner(jnp.where(first, right_half, left_half), "row", 1)
    rhs_pair = in_order(jnp.where(first, left_half, right_half), rhs_theirs, 1)
    places = jnp.stack([chip, core, leaf]).astype(jnp.int32)
    scalars = [jnp.concatenate([places, widths[:, 0]]), structure[0]]

    folded_at = {}

    def fold(pairs, picked, blocks, levels, keep):
        cursor, spans = 0, []
        for s, t in pairs:
            folded_at[s, t] = cursor
            spans.append((s, offsets[s, t], group[t]))
            cursor += group[t]
        mine, half, *held = fold_blocks(
            scalars,
            factor[0],
            diag_inverse[0],
            spans,
            [pairs.index(picked)],
            blocks,
            levels,
            keep,
        )
        theirs = from_partner(mine, "row", 1)
        return (mine, theirs), half, held

    lowest = [(0, 1), (0, 2)]
    folded_first, lower_half, _ = fold(lowest, (0, 1), group[1] + group[2], 1, False)
    others = sorted([(s, s + 1) for s in range(1, top)] + [(1, 3)])
    folded, upper_half, (own_blocks, inverses) = fold(others, (1, 2), factor.shape[1], levels, True)
    their_blocks = from_partner(factor[0], "row", 1)
    sides = [own_blocks, their_blocks]
    lower_mine = gather_chips(lower_half)
    upper = [upper_half] + exchange_leaves([upper_half] * (group[1] - 1))

    def skip_product(lower_mine, upper, after):
        lower_mine, upper, _ = lax.optimization_barrier((lower_mine, upper, after))
        lower_theirs = from_partner(jnp.stack(lower_mine), "row", 1)
        (mine,) = skip_level(scalars, upper, lower_mine, lower_theirs, folded_first[0], folded_at[0, 2])
        theirs = from_partner(mine, "row", 1)
        return mine, theirs

    pending = {t: None for t in range(levels)}
    turned, kept, sent = [None] * levels, [None] * levels, [None] * levels

    def finish_level(l, parts):
        later = list(range(l + 2, levels))
        before = None if l == 0 else [pending[t] for t in later]
        spans = [(offsets[l, t], group[t]) for t in later]
        turned[l], kept[l], sent[l], *after = finish(
            scalars, l, parts, inverses, sides, spans, before
        )
        pending.update(zip(later, after))

    def push_level(l, parts):
        pair, at = folded if l else folded_first, folded_at[l, l + 1]
        return push(scalars, parts, full, group[l + 1], pending[l + 1], pair, at)

    parts = gather_chips(rhs_pair[0])
    own, *messages = push_level(0, parts)
    for l in range(1, levels):
        received = exchange_leaves(messages)
        finish_level(l - 1, parts)
        update = own
        for piece in received:
            update = update + piece.astype(F32)
        now = (rhs_pair[l].astype(F32) - update).astype(BF16)
        parts = gather_chips(now)
        if l < top:
            own, *messages = push_level(l, parts)
        if l == SKIP_LEVEL:
            skip = skip_product(lower_mine, upper, own)
    finish_level(top, parts)

    adjoint = [None] * levels

    def gather_leaves(named):
        span = max(group[l] for l, _ in named)
        listed = [[i for i, (l, _) in enumerate(named) if group[l] > k] for k in range(span)]
        stacks = [jnp.stack([named[i][1] for i in row]) for row in listed]
        pieces = [stacks[0]] + exchange_leaves(stacks[1:])
        vectors = [
            [(k, listed[k].index(i)) for k in range(group[l])] for i, (l, _) in enumerate(named)
        ]
        return pieces, vectors

    def total_of(own, received, slot):
        total = own[slot]
        for piece in received:
            total = total + piece[slot].astype(F32)
        return total

    adjoint[top] = turned[top].astype(BF16)
    pieces, vectors = gather_leaves([(top, adjoint[top])])
    sums = {s: None for s in range(levels)}
    for l in range(top - 1, 1, -1):
        t = l + 1
        outputs = [([(0, 0, folded_at[l, t])], sums[l])]
        if l == 2:
            outputs.append(([(0, 0, folded_at[1, t])], sums[1]))
        own, *messages = pull(scalars, pieces, vectors, outputs, [folded], full, chips)
        received = exchange_chips(messages)
        sources = [s for s in range(t - 1) if (s, t) != (1, 3)]
        complete = {t - 2} if t > 4 else {1, 2} if t == 4 else {0}
        listed = [(s, [(0, offsets[s, t])], sums[s], s in complete) for s in sources]
        sums.update(zip(sources, pull_rest(scalars, pieces, vectors, listed, sides, inverses)))
        adjoint[l] = (turned[l] - total_of(own, received, 0)).astype(BF16)
        named = [(l, adjoint[l])]
        if l == 2:
            ahead = turned[1] - total_of(own, received, 1)
            named.append((1, ahead.astype(BF16)))
        pieces, vectors = gather_leaves(named)
    outputs = [
        ([(0, 1, 0), (1, 2, folded_at[0, 1])], sums[0]),
        ([(0, 0, folded_at[1, 2])], None),
    ]
    own, *messages = pull(scalars, pieces, vectors, outputs, [folded, skip, folded_first], full, chips)
    received = exchange_chips(messages)
    adjoint[0] = (turned[0] - total_of(own, received, 0)).astype(BF16)
    adjoint[1] = (ahead - total_of(own, received, 1)).astype(BF16)

    theirs = from_partner(jnp.stack(sent), "row", 1)
    forward = in_order(jnp.stack(kept), theirs, 2)

    def swap_rows(values):
        stacked = jnp.stack(values)
        low_rows, high_rows = stacked[:, :block_rows], stacked[:, block_rows:]
        theirs = from_partner(jnp.where(first, high_rows, low_rows), "row", 1)
        return in_order(jnp.where(first, low_rows, high_rows), theirs, 2)

    upper_levels = swap_rows(adjoint[2:])
    backward = jnp.concatenate([swap_rows(adjoint[:2]), upper_levels])
    return forward[:, None], backward[:, None]


def solution(mesh):
    placed = (
        P(None, "leaf", "row", None),
        P("leaf", None, None, None),
        P("leaf", None, "row", None),
        P(None, "leaf"),
        P("leaf", None),
    )

    def solve(rhs, diag_inverse, factor, widths, structure):
        step = jax.shard_map(
            shards,
            mesh=mesh,
            in_specs=placed,
            out_specs=(P(None, "leaf", "row", None), P(None, "leaf", "row", None)),
            check_vma=False,
        )
        return step(
            rhs, diag_inverse, factor, widths, structure
        )

    return solve
```

time: 182 us -> 185 us (1.016)
  waiting for transfers between devices: 65.2 us -> 40.5 us
  Pallas kernels: 22.3 us -> 41.6 us
  starting transfers between devices: 82.3 us -> 86.6 us
  local copies, waits for them, and re-layouts: 8.06 us -> 11.2 us
    ppermute x63 -> x68, waiting for transfers between devices: 65.2 us -> 40.5 us  [from_partner(): lax.ppermute(x, axis, [(i, i ^ mask) for i in range(lax.axis_size(axis))])]
    pallas_call x18 -> x17, Pallas kernels: 22.3 us -> 41.6 us  [call(): pl.pallas_call(body, out_shape=[jax.ShapeDtypeStruct(s, d) for s, d in ou...]
    pallas_call x4, local copies, waits for them, and re-layouts: 3.84 us -> 8.6 us  [call(): pl.pallas_call(body, out_shape=[jax.ShapeDtypeStruct(s, d) for s, d in ou...]
    ppermute x63 -> x68, starting transfers between devices: 82.3 us -> 86.6 us  [from_partner(): lax.ppermute(x, axis, [(i, i ^ mask) for i in range(lax.axis_size(axis))])]
    squeeze x2 -> x1, local copies, waits for them, and re-layouts: 2.04 us -> 0.01 us  [shards(): parts = gather_chips(rhs_pair[0])]
  transfers between devices with their start and end apart: 63 -> 68, of which waited for: 45 -> 31; matrix products, arithmetic and copies ran while one was open for 4% -> 6% of each run, Pallas kernels for 5% -> 17%
where the time goes in v1:
time: 185 us
  starting transfers between devices  86.6 us (47%)
  Pallas kernels  41.6 us (22%)
  waiting for transfers between devices  40.5 us (22%)
  local copies, waits for them, and re-layouts  11.2 us (6%)
  other arithmetic  3.63 us (2%)
    ppermute x68, starting transfers between devices, from_partner(): lax.ppermute(x, axis, [(i, i ^ mask) for i in range(lax.axis_size(axis))])  86.6 us
    pallas_call x17, Pallas kernels, call(): pl.pallas_call(body, out_shape=[jax.ShapeDtypeStruct(s, d) for s, d in ou...  41.6 us
    ppermute x68, waiting for transfers between devices, from_partner(): lax.ppermute(x, axis, [(i, i ^ mask) for i in range(lax.axis_size(axis))])  40.5 us
    pallas_call x4, local copies, waits for them, and re-layouts, call(): pl.pallas_call(body, out_shape=[jax.ShapeDtypeStruct(s, d) for s, d in ou...  8.6 us
  transfers between devices with their start and end apart: 68, of which 31 were waited for; matrix products, arithmetic and copies ran while one was open for 6% of the time, Pallas kernels for 17%

profile of v1, /device:TPU:0, one launch (start us, length us, event | category | flops | bytes accessed | tf_op | source)
XLA Modules:
  0.0 184.7 jit_solution(5729662988584611038)
XLA Ops:
  2.6 5.7 %shard_map.68 = (bf16[20,64,512]{2,1,0:T(8,128)(2,1)}, bf16[4,64,512]{2,1,0:T(8,128)(2,1)S(1)}, bf16[58,64,512]{2,1,0:T(8,128)(2,1)S(1)}, bf16[6,512,512]{2,1,0:T(8,128)(2,1)S(1)}) custom-call(s32[9]{0:T(128)S(1)} %pad_add_fusion.s, s32[58]{0:T(128)S(1)} %bitcast.126, bf16[58,64,512]{2,1,0:T(8,128)(2,1)} %bitcast.138, bf16[6,512,512]{2,1,0:T(8,128)(2,1)} %bitcast.140), custom_call_target="tpu_custom_call" | custom-call | tf_op jit(solution)/shard_map/pallas_call | solution.py:48
  11.8 2.3 %shard_map.70 = (bf16[6,64,512]{2,1,0:T(8,128)(2,1)S(1)}, bf16[2,64,512]{2,1,0:T(8,128)(2,1)S(1)}) custom-call(s32[9]{0:T(128)S(1)} %pad_add_fusion.s, s32[58]{0:T(128)S(1)} %bitcast.127, bf16[58,64,512]{2,1,0:T(8,128)(2,1)} %bitcast.139, bf16[6,512,512]{2,1,0:T(8,128)(2,1)} %bitcast.141), custom_call_target="tpu_custom_call" | custom-call | tf_op jit(solution)/shard_map/pallas_call | solution.py:48
  14.6 2.8 %collective-permute-start.1 = (bf16[128,128]{1,0:T(8,128)(2,1)S(1)}, bf16[128,128]{1,0:T(8,128)(2,1)S(1)}, u32[]{:S(2)}, u32[]{:S(2)}) collective-permute-start(bf16[128,128]{1,0:T(8,128)(2,1)S(1)} %slice_bitcast_fusion.5.refs_0_), channel_id=1, source_target_pairs={{0,2},{1,3},{2,0},{3,1},{4,6},{5,7},{6,4},{7,5},{8,10},{9,11},{10,... | collective-permute-start | bytes 98312 | tf_op jit(solution)/shard_map/ppermute | solution.py:24
  17.4 2.6 %collective-permute-start.2 = (bf16[128,128]{1,0:T(8,128)(2,1)S(1)}, bf16[128,128]{1,0:T(8,128)(2,1)S(1)}, u32[]{:S(2)}, u32[]{:S(2)}) collective-permute-start(bf16[128,128]{1,0:T(8,128)(2,1)S(1)} %slice_bitcast_fusion.5.refs_0_), channel_id=1, source_target_pairs={{0,4},{1,5},{2,6},{3,7},{4,0},{5,1},{6,2},{7,3},{8,12},{9,13},{10,... | collective-permute-start | bytes 98312 | tf_op jit(solution)/shard_map/ppermute | solution.py:24
  20.0 3.3 %collective-permute-start.3 = (bf16[128,128]{1,0:T(8,128)(2,1)S(1)}, bf16[128,128]{1,0:T(8,128)(2,1)S(1)}, u32[]{:S(2)}, u32[]{:S(2)}) collective-permute-start(bf16[128,128]{1,0:T(8,128)(2,1)S(1)} %slice_bitcast_fusion.5.refs_0_), channel_id=1, source_target_pairs={{0,6},{1,7},{2,4},{3,5},{4,2},{5,3},{6,0},{7,1},{8,14},{9,15},{10,... | collective-permute-start | bytes 98312 | tf_op jit(solution)/shard_map/ppermute | solution.py:24
  23.3 2.4 %collective-permute-done.3.refs_3_ = bf16[128,128]{1,0:T(8,128)(2,1)S(1)} collective-permute-done((bf16[128,128]{1,0:T(8,128)(2,1)S(1)}, bf16[128,128]{1,0:T(8,128)(2,1)S(1)}, u32[]{:S(2)}, u32[]{:S(2)}) %collective-permute-start.3) | collective-permute-done | bytes 32800 | tf_op jit(solution)/shard_map/ppermute | solution.py:24
  28.1 2.4 %collective-permute-done.6 = bf16[128,128]{1,0:T(8,128)(2,1)S(1)} collective-permute-done((bf16[128,128]{1,0:T(8,128)(2,1)S(1)}, bf16[128,128]{1,0:T(8,128)(2,1)S(1)}, u32[]{:S(2)}, u32[]{:S(2)}) %collective-permute-start.6) | collective-permute-done | bytes 32800 | tf_op jit(solution)/shard_map/ppermute | solution.py:24
  30.6 3.9 %collective-permute-start.8 = (bf16[128,128]{1,0:T(8,128)(2,1)S(1)}, bf16[128,128]{1,0:T(8,128)(2,1)S(1)}, u32[]{:S(2)}, u32[]{:S(2)}) collective-permute-start(bf16[128,128]{1,0:T(8,128)(2,1)S(1)} %fusion.5.refs_0_), channel_id=1, source_target_pairs={{0,4},{1,5},{2,6},{3,7},{4,0},{5,1},{6,2},{7,3},{8,12},{9,13},{10,... | collective-permute-start | bytes 98312 | tf_op jit(solution)/shard_map/ppermute | solution.py:24
  35.0 3.4 %shard_map.69 = (f32[128,128]{1,0:T(8,128)S(1)}, bf16[64,128]{1,0:T(8,128)(2,1)S(1)}, bf16[64,128]{1,0:T(8,128)(2,1)S(1)}, f32[4,128,128]{2,1,0:T(8,128)S(1)}, f...) custom-call(s32[9]{0:T(128)S(1)} %pad_add_fusion.s, s32[58]{0:T(128)S(1)} %bitcast.128, ...), custom_call_target="tpu_custom_call" | custom-call | tf_op jit(solution)/shard_map/pallas_call | solution.py:48
  47.7 2.4 %collective-permute-done.13 = bf16[128,128]{1,0:T(8,128)(2,1)S(1)} collective-permute-done((bf16[128,128]{1,0:T(8,128)(2,1)S(1)}, bf16[128,128]{1,0:T(8,128)(2,1)S(1)}, u32[]{:S(2)}, u32[]{:S(2)}) %collective-permute-start.13) | collective-permute-done | bytes 32800 | tf_op jit(solution)/shard_map/ppermute | solution.py:24
  52.4 2.3 %collective-permute-start.16 = (bf16[128,128]{1,0:T(8,128)(2,1)S(1)}, bf16[128,128]{1,0:T(8,128)(2,1)S(1)}, u32[]{:S(2)}, u32[]{:S(2)}) collective-permute-start(bf16[128,128]{1,0:T(8,128)(2,1)S(1)} %fusion.4.refs_0_), channel_id=1, source_target_pairs={{0,6},{1,7},{2,4},{3,5},{4,2},{5,3},{6,0},{7,1},{8,14},{9,15},{10,... | collective-permute-start | bytes 98312 | tf_op jit(solution)/shard_map/ppermute | solution.py:24
  54.6 3.3 %shard_map.72 = (f32[128,128]{1,0:T(8,128)S(1)}, bf16[64,128]{1,0:T(8,128)(2,1)S(1)}, bf16[64,128]{1,0:T(8,128)(2,1)S(1)}, f32[4,128,128]{2,1,0:T(8,128)S(1)}, f...) custom-call(s32[9]{0:T(128)S(1)} %pad_add_fusion.s, s32[58]{0:T(128)S(1)} %bitcast.129, ...), custom_call_target="tpu_custom_call" | custom-call | tf_op jit(solution)/shard_map/pallas_call | solution.py:48
  61.2 2.4 %collective-permute-start.19 = (bf16[128,128]{1,0:T(8,128)(2,1)S(1)}, bf16[128,128]{1,0:T(8,128)(2,1)S(1)}, u32[]{:S(2)}, u32[]{:S(2)}) collective-permute-start(bf16[128,128]{1,0:T(8,128)(2,1)S(1)} %get-tuple-element.106), channel_id=1, source_target_pairs={{0,24},{8,16},{16,8},{24,0},{1,25},{9,17},{17,9},{25,1},{2,26},{10... | collective-permute-start | bytes 98312 | tf_op jit(solution)/shard_map/ppermute | solution.py:24
  66.1 2.8 %collective-permute-start.21 = (bf16[128,128]{1,0:T(8,128)(2,1)S(1)}, bf16[128,128]{1,0:T(8,128)(2,1)S(1)}, u32[]{:S(2)}, u32[]{:S(2)}) collective-permute-start(bf16[128,128]{1,0:T(8,128)(2,1)S(1)} %fusion.3.refs_0_), channel_id=1, source_target_pairs={{0,4},{1,5},{2,6},{3,7},{4,0},{5,1},{6,2},{7,3},{8,12},{9,13},{10,... | collective-permute-start | bytes 98312 | tf_op jit(solution)/shard_map/ppermute | solution.py:24
  70.5 3.1 %shard_map.88 = (bf16[6,64,128]{2,1,0:T(8,128)(2,1)S(1)}, f32[4,128,128]{2,1,0:T(8,128)S(1)}, f32[4,128,128]{2,1,0:T(8,128)S(1)}, bf16[64,128]{1,0:T(8,128)(2,1)S(1)}, f32[128,128]{1,0:T(8,128)S(1)}) fusion(bf16[6,64,128]{2,1,0:T(8,128)(2,1)S(1)} %constant_dynamic-update-slice_fusion.4, s32[9]{0:T(128)S(1)} %pad_add_fusion.s, s32[58]{0:T(128)S(1)} %bitcast.130, ...), kind=kCustom, calls=%fused_computation.56 | custom fusion | bytes 12026880 | tf_op jit(solution)/shard_map/pallas_call | solution.py:48
  82.9 2.2 %collective-permute-done.25 = bf16[128,128]{1,0:T(8,128)(2,1)S(1)} collective-permute-done((bf16[128,128]{1,0:T(8,128)(2,1)S(1)}, bf16[128,128]{1,0:T(8,128)(2,1)S(1)}, u32[]{:S(2)}, u32[]{:S(2)}) %collective-permute-start.25) | collective-permute-done | bytes 32800 | tf_op jit(solution)/shard_map/ppermute | solution.py:24
  85.2 2.2 %collective-permute-start.27 = (bf16[128,128]{1,0:T(8,128)(2,1)S(1)}, bf16[128,128]{1,0:T(8,128)(2,1)S(1)}, u32[]{:S(2)}, u32[]{:S(2)}) collective-permute-start(bf16[128,128]{1,0:T(8,128)(2,1)S(1)} %fusion.2.refs_0_), channel_id=1, source_target_pairs={{0,4},{1,5},{2,6},{3,7},{4,0},{5,1},{6,2},{7,3},{8,12},{9,13},{10,... | collective-permute-start | bytes 98312 | tf_op jit(solution)/shard_map/ppermute | solution.py:24
  89.5 3.0 %shard_map.87 = (bf16[6,64,128]{2,1,0:T(8,128)(2,1)S(1)}, f32[4,128,128]{2,1,0:T(8,128)S(1)}, bf16[64,128]{1,0:T(8,128)(2,1)S(1)}, f32[128,128]{1,0:T(8,128)S(1)}) fusion(bf16[6,64,128]{2,1,0:T(8,128)(2,1)S(1)} %get-tuple-element.176, s32[9]{0:T(128)S(1)} %pad_add_fusion.s, s32[58]{0:T(128)S(1)} %bitcast.131, bf16[128,128]{1,0:T(8,128)(2,1)S(1)} %fusion.3.refs_0_, ...), kind=kCustom, calls=%fused_computation.55 | custom fusion | bytes 11502592 | tf_op jit(solution)/shard_map/pallas_call | solution.py:48
  96.6 2.2 %collective-permute-start.31 = (bf16[128,128]{1,0:T(8,128)(2,1)S(1)}, bf16[128,128]{1,0:T(8,128)(2,1)S(1)}, u32[]{:S(2)}, u32[]{:S(2)}) collective-permute-start(bf16[128,128]{1,0:T(8,128)(2,1)S(1)} %get-tuple-element.119), channel_id=1, source_target_pairs={{0,24},{8,16},{16,8},{24,0},{1,25},{9,17},{17,9},{25,1},{2,26},{10... | collective-permute-start | bytes 98312 | tf_op jit(solution)/shard_map/ppermute | solution.py:24
  101.5 2.6 %collective-permute-start.33 = (bf16[128,128]{1,0:T(8,128)(2,1)S(1)}, bf16[128,128]{1,0:T(8,128)(2,1)S(1)}, u32[]{:S(2)}, u32[]{:S(2)}) collective-permute-start(bf16[128,128]{1,0:T(8,128)(2,1)S(1)} %fusion.1), channel_id=1, source_target_pairs={{0,4},{1,5},{2,6},{3,7},{4,0},{5,1},{6,2},{7,3},{8,12},{9,13},{10,... | collective-permute-start | bytes 98312 | tf_op jit(solution)/shard_map/ppermute | solution.py:24
  123.3 2.3 %collective-permute-start.41 = (bf16[1,128,128]{2,1,0:T(8,128)(2,1)S(1)}, bf16[1,128,128]{2,1,0:T(8,128)(2,1)S(1)}, u32[]{:S(2)}, u32[]{:S(2)}) collective-permute-start(bf16[1,128,128]{2,1,0:T(8,128)(2,1)S(1)} %get-tuple-element.135), channel_id=1, source_target_pairs={{0,6},{1,7},{2,4},{3,5},{4,2},{5,3},{6,0},{7,1},{8,14},{9,15},{10,... | collective-permute-start | bytes 98312 | tf_op jit(solution)/shard_map/ppermute | solution.py:24
  126.1 2.9 %collective-permute-done.41 = bf16[1,128,128]{2,1,0:T(8,128)(2,1)S(1)} collective-permute-done((bf16[1,128,128]{2,1,0:T(8,128)(2,1)S(1)}, bf16[1,128,128]{2,1,0:T(8,128)(2,1)S(1)}, u32[]{:S(2)}, u32[]{:S(2)}) %collective-permute-start.41) | collective-permute-done | bytes 32800 | tf_op jit(solution)/shard_map/ppermute | solution.py:24
  132.6 2.8 %shard_map.78 = (f32[128,512]{1,0:T(8,128)S(1)}, f32[128,512]{1,0:T(8,128)S(1)}, f32[128,512]{1,0:T(8,128)S(1)}, f32[128,512]{1,0:T(8,128)S(1)}) custom-call(s32[9]{0:T(128)S(1)} %pad_add_fusion.s, s32[58]{0:T(128)S(1)} %bitcast.134, bf16[1,128,128]{2,1,0:T(8,128)(2,1)S(1)} %convert_bitcast_fusion.1.refs_0_, ...), custom_call_target="tpu_custom_call" | custom-call | tf_op jit(solution)/shard_map/pallas_call | solution.py:48
  137.9 3.3 %collective-permute-start.46 = (bf16[1,128,128]{2,1,0:T(8,128)(2,1)S(1)}, bf16[1,128,128]{2,1,0:T(8,128)(2,1)S(1)}, u32[]{:S(2)}, u32[]{:S(2)}) collective-permute-start(bf16[1,128,128]{2,1,0:T(8,128)(2,1)S(1)} %get-tuple-element.139), channel_id=1, source_target_pairs={{0,4},{1,5},{2,6},{3,7},{4,0},{5,1},{6,2},{7,3},{8,12},{9,13},{10,... | collective-permute-start | bytes 98312 | tf_op jit(solution)/shard_map/ppermute | solution.py:24
  143.1 3.8 %collective-permute-done.47 = bf16[1,128,128]{2,1,0:T(8,128)(2,1)S(1)} collective-permute-done((bf16[1,128,128]{2,1,0:T(8,128)(2,1)S(1)}, bf16[1,128,128]{2,1,0:T(8,128)(2,1)S(1)}, u32[]{:S(2)}, u32[]{:S(2)}) %collective-permute-start.47) | collective-permute-done | bytes 32800 | tf_op jit(solution)/shard_map/ppermute | solution.py:24
  150.5 2.9 %shard_map.80 = (f32[128,512]{1,0:T(8,128)S(1)}, f32[128,512]{1,0:T(8,128)S(1)}, f32[128,512]{1,0:T(8,128)S(1)}) custom-call(s32[9]{0:T(128)S(1)} %pad_add_fusion.s, s32[58]{0:T(128)S(1)} %bitcast.135, bf16[1,128,128]{2,1,0:T(8,128)(2,1)S(1)} %fusion.11.refs_0_, bf16[1,128,128]{2,1,0:T(8,128)(2,1)S(1)} %collective-permute-done.42.refs_1_, ...), custom_call_target="tpu_custom_call" | custom-call | tf_op jit(solution)/shard_map/pallas_call | solution.py:48
  153.6 2.2 %shard_map.81 = (f32[2,128,128]{2,1,0:T(8,128)S(1)}, bf16[2,128,128]{2,1,0:T(8,128)(2,1)S(1)}, bf16[2,128,128]{2,1,0:T(8,128)(2,1)S(1)}, bf16[2,128,128]{2,1,0:T(8,128)(2,1)S(1)}) custom-call(s32[9]{0:T(128)S(1)} %pad_add_fusion.s, bf16[1,128,128]{2,1,0:T(8,128)(2,1)S(1)} %fusion.12.refs_0_, bf16[1,128,128]{2,1,0:T(8,128)(2,1)S(1)} %collective-permute-done.48.refs_1_, ...), custom_call_target="tpu_custom_call" | custom-call | tf_op jit(solution)/shard_map/pallas_call | solution.py:48
  158.0 2.3 %collective-permute-start.53 = (bf16[2,128,128]{2,1,0:T(8,128)(2,1)S(1)}, bf16[2,128,128]{2,1,0:T(8,128)(2,1)S(1)}, u32[]{:S(2)}, u32[]{:S(2)}) collective-permute-start(bf16[2,128,128]{2,1,0:T(8,128)(2,1)S(1)} %get-tuple-element.149), channel_id=1, source_target_pairs={{0,6},{1,7},{2,4},{3,5},{4,2},{5,3},{6,0},{7,1},{8,14},{9,15},{10,... | collective-permute-start | bytes 196616 | tf_op jit(solution)/shard_map/ppermute | solution.py:24
  161.0 2.5 %shard_map.83.refs_10_ = f32[128,512]{1,0:T(8,128)S(1)} custom-call(s32[9]{0:T(128)S(1)} %pad_add_fusion.s, s32[58]{0:T(128)S(1)} %bitcast.136, bf16[1,128,128]{2,1,0:T(8,128)(2,1)S(1)} %fusion.12.refs_0_, bf16[1,128,128]{2,1,0:T(8,128)(2,1)S(1)} %collective-permute-done.48.refs_1_, bf16[1,128,128]{2,1,0:T(8,128)(2,1)S(1)} %collective-permute-done.49.refs_2_, ...), custom_call_target="tpu_custom_call" | custom-call | tf_op jit(solution)/shard_map/pallas_call | solution.py:48
  171.9 2.3 %shard_map.84 = (f32[2,128,128]{2,1,0:T(8,128)S(1)}, bf16[2,128,128]{2,1,0:T(8,128)(2,1)S(1)}, bf16[2,128,128]{2,1,0:T(8,128)(2,1)S(1)}, bf16[2,128,128]{2,1,0:T(8,128)(2,1)S(1)}) custom-call(s32[9]{0:T(128)S(1)} %pad_add_fusion.s, bf16[2,128,128]{2,1,0:T(8,128)(2,1)S(1)} %pad_maximum_fusion.2.refs_0_, ...), custom_call_target="tpu_custom_call" | custom-call | tf_op jit(solution)/shard_map/pallas_call | solution.py:48
  174.3 2.3 %collective-permute-start.64 = (bf16[2,128,128]{2,1,0:T(8,128)(2,1)S(1)}, bf16[2,128,128]{2,1,0:T(8,128)(2,1)S(1)}, u32[]{:S(2)}, u32[]{:S(2)}) collective-permute-start(bf16[2,128,128]{2,1,0:T(8,128)(2,1)S(1)} %get-tuple-element.162), channel_id=1, source_target_pairs={{0,4},{1,5},{2,6},{3,7},{4,0},{5,1},{6,2},{7,3},{8,12},{9,13},{10,... | collective-permute-start | bytes 196616 | tf_op jit(solution)/shard_map/ppermute | solution.py:24
  178.8 2.3 %collective-permute-done.64 = bf16[2,128,128]{2,1,0:T(8,128)(2,1)S(1)} collective-permute-done((bf16[2,128,128]{2,1,0:T(8,128)(2,1)S(1)}, bf16[2,128,128]{2,1,0:T(8,128)(2,1)S(1)}, u32[]{:S(2)}, u32[]{:S(2)}) %collective-permute-start.64) | collective-permute-done | bytes 65568 | tf_op jit(solution)/shard_map/ppermute | solution.py:24
  (164 shorter events, 94.2 us)
Async XLA Ops:
  0.6 34.3 %collective-permute-start.4 = (bf16[58,64,512]{2,1,0:T(8,128)(2,1)}, bf16[58,64,512]{2,1,0:T(8,128)(2,1)}, u32[]{:S(2)}, u32[]{:S(2)}) collective-permute-start(bf16[58,64,512]{2,1,0:T(8,128)(2,1)} %bitcast.137), channel_id=1, source_target_pairs={{0,1},{1,0},{2,3},{3,2},{4,5},{5,4},{6,7},{7,6},{8,9},{9,8},{10,11... | collective-permute-start | bytes 11403272 | tf_op jit(solution)/shard_map/ppermute | solution.py:24
  10.2 29.9 %collective-permute-start.10 = (bf16[20,64,512]{2,1,0:T(8,128)(2,1)}, bf16[20,64,512]{2,1,0:T(8,128)(2,1)}, u32[]{:S(2)}, u32[]{:S(2)}) collective-permute-start(bf16[20,64,512]{2,1,0:T(8,128)(2,1)} %get-tuple-element.93.refs_4_), channel_id=1, source_target_pairs={{0,1},{1,0},{2,3},{3,2},{4,5},{5,4},{6,7},{7,6},{8,9},{9,8},{10,11... | collective-permute-start | bytes 3932168 | tf_op jit(solution)/shard_map/ppermute | solution.py:24
  14.1 11.6 %collective-permute-start.5 = (bf16[6,64,512]{2,1,0:T(8,128)(2,1)S(1)}, bf16[6,64,512]{2,1,0:T(8,128)(2,1)S(1)}, u32[]{:S(2)}, u32[]{:S(2)}) collective-permute-start(bf16[6,64,512]{2,1,0:T(8,128)(2,1)S(1)} %get-tuple-element.86.refs_4_.refs_7_.refs_8_), channel_id=1, source_target_pairs={{0,1},{1,0},{2,3},{3,2},{4,5},{5,4},{6,7},{7,6},{8,9},{9,8},{10,11... | collective-permute-start | bytes 1179656 | tf_op jit(solution)/shard_map/ppermute | solution.py:24
  17.4 5.9 %collective-permute-start.2 = (bf16[128,128]{1,0:T(8,128)(2,1)S(1)}, bf16[128,128]{1,0:T(8,128)(2,1)S(1)}, u32[]{:S(2)}, u32[]{:S(2)}) collective-permute-start(bf16[128,128]{1,0:T(8,128)(2,1)S(1)} %slice_bitcast_fusion.5.refs_0_), channel_id=1, source_target_pairs={{0,4},{1,5},{2,6},{3,7},{4,0},{5,1},{6,2},{7,3},{8,12},{9,13},{10,... | collective-permute-start | bytes 98312 | tf_op jit(solution)/shard_map/ppermute | solution.py:24
  30.5 7.9 %collective-permute-start.7 = (bf16[128,128]{1,0:T(8,128)(2,1)S(1)}, bf16[128,128]{1,0:T(8,128)(2,1)S(1)}, u32[]{:S(2)}, u32[]{:S(2)}) collective-permute-start(bf16[128,128]{1,0:T(8,128)(2,1)S(1)} %fusion.5.refs_0_), channel_id=1, source_target_pairs={{0,2},{1,3},{2,0},{3,1},{4,6},{5,7},{6,4},{7,5},{8,10},{9,11},{10,... | collective-permute-start | bytes 98312 | tf_op jit(solution)/shard_map/ppermute | solution.py:24
  30.6 7.8 %collective-permute-start.8 = (bf16[128,128]{1,0:T(8,128)(2,1)S(1)}, bf16[128,128]{1,0:T(8,128)(2,1)S(1)}, u32[]{:S(2)}, u32[]{:S(2)}) collective-permute-start(bf16[128,128]{1,0:T(8,128)(2,1)S(1)} %fusion.5.refs_0_), channel_id=1, source_target_pairs={{0,4},{1,5},{2,6},{3,7},{4,0},{5,1},{6,2},{7,3},{8,12},{9,13},{10,... | collective-permute-start | bytes 98312 | tf_op jit(solution)/shard_map/ppermute | solution.py:24
  50.2 7.7 %collective-permute-start.14 = (bf16[128,128]{1,0:T(8,128)(2,1)S(1)}, bf16[128,128]{1,0:T(8,128)(2,1)S(1)}, u32[]{:S(2)}, u32[]{:S(2)}) collective-permute-start(bf16[128,128]{1,0:T(8,128)(2,1)S(1)} %fusion.4.refs_0_), channel_id=1, source_target_pairs={{0,2},{1,3},{2,0},{3,1},{4,6},{5,7},{6,4},{7,5},{8,10},{9,11},{10,... | collective-permute-start | bytes 98312 | tf_op jit(solution)/shard_map/ppermute | solution.py:24
  50.2 7.7 %collective-permute-start.15 = (bf16[128,128]{1,0:T(8,128)(2,1)S(1)}, bf16[128,128]{1,0:T(8,128)(2,1)S(1)}, u32[]{:S(2)}, u32[]{:S(2)}) collective-permute-start(bf16[128,128]{1,0:T(8,128)(2,1)S(1)} %fusion.4.refs_0_), channel_id=1, source_target_pairs={{0,4},{1,5},{2,6},{3,7},{4,0},{5,1},{6,2},{7,3},{8,12},{9,13},{10,... | collective-permute-start | bytes 98312 | tf_op jit(solution)/shard_map/ppermute | solution.py:24
  66.1 7.6 %collective-permute-start.20 = (bf16[128,128]{1,0:T(8,128)(2,1)S(1)}, bf16[128,128]{1,0:T(8,128)(2,1)S(1)}, u32[]{:S(2)}, u32[]{:S(2)}) collective-permute-start(bf16[128,128]{1,0:T(8,128)(2,1)S(1)} %fusion.3.refs_0_), channel_id=1, source_target_pairs={{0,2},{1,3},{2,0},{3,1},{4,6},{5,7},{6,4},{7,5},{8,10},{9,11},{10,... | collective-permute-start | bytes 98312 | tf_op jit(solution)/shard_map/ppermute | solution.py:24
  66.1 7.5 %collective-permute-start.21 = (bf16[128,128]{1,0:T(8,128)(2,1)S(1)}, bf16[128,128]{1,0:T(8,128)(2,1)S(1)}, u32[]{:S(2)}, u32[]{:S(2)}) collective-permute-start(bf16[128,128]{1,0:T(8,128)(2,1)S(1)} %fusion.3.refs_0_), channel_id=1, source_target_pairs={{0,4},{1,5},{2,6},{3,7},{4,0},{5,1},{6,2},{7,3},{8,12},{9,13},{10,... | collective-permute-start | bytes 98312 | tf_op jit(solution)/shard_map/ppermute | solution.py:24
  69.0 6.2 %collective-permute-start.22 = (bf16[128,128]{1,0:T(8,128)(2,1)S(1)}, bf16[128,128]{1,0:T(8,128)(2,1)S(1)}, u32[]{:S(2)}, u32[]{:S(2)}) collective-permute-start(bf16[128,128]{1,0:T(8,128)(2,1)S(1)} %fusion.3.refs_0_), channel_id=1, source_target_pairs={{0,6},{1,7},{2,4},{3,5},{4,2},{5,3},{6,0},{7,1},{8,14},{9,15},{10,... | collective-permute-start | bytes 98312 | tf_op jit(solution)/shard_map/ppermute | solution.py:24
  80.7 32.3 %collective-permute-start.57 = (bf16[2,64,512]{2,1,0:T(8,128)(2,1)S(1)}, bf16[2,64,512]{2,1,0:T(8,128)(2,1)S(1)}, u32[]{:S(2)}, u32[]{:S(2)}) collective-permute-start(bf16[2,64,512]{2,1,0:T(8,128)(2,1)S(1)} %get-tuple-element.155.refs_2_), channel_id=1, source_target_pairs={{0,2},{1,3},{2,0},{3,1},{4,6},{5,7},{6,4},{7,5},{8,10},{9,11},{10,... | collective-permute-start | bytes 393224 | tf_op jit(solution)/shard_map/ppermute | solution.py:24
  80.7 33.5 %collective-permute-start.58 = (bf16[2,64,512]{2,1,0:T(8,128)(2,1)S(1)}, bf16[2,64,512]{2,1,0:T(8,128)(2,1)S(1)}, u32[]{:S(2)}, u32[]{:S(2)}) collective-permute-start(bf16[2,64,512]{2,1,0:T(8,128)(2,1)S(1)} %get-tuple-element.155.refs_2_), channel_id=1, source_target_pairs={{0,4},{1,5},{2,6},{3,7},{4,0},{5,1},{6,2},{7,3},{8,12},{9,13},{10,... | collective-permute-start | bytes 393224 | tf_op jit(solution)/shard_map/ppermute | solution.py:24
  85.1 7.4 %collective-permute-start.26 = (bf16[128,128]{1,0:T(8,128)(2,1)S(1)}, bf16[128,128]{1,0:T(8,128)(2,1)S(1)}, u32[]{:S(2)}, u32[]{:S(2)}) collective-permute-start(bf16[128,128]{1,0:T(8,128)(2,1)S(1)} %fusion.2.refs_0_), channel_id=1, source_target_pairs={{0,2},{1,3},{2,0},{3,1},{4,6},{5,7},{6,4},{7,5},{8,10},{9,11},{10,... | collective-permute-start | bytes 98312 | tf_op jit(solution)/shard_map/ppermute | solution.py:24
  85.2 7.4 %collective-permute-start.27 = (bf16[128,128]{1,0:T(8,128)(2,1)S(1)}, bf16[128,128]{1,0:T(8,128)(2,1)S(1)}, u32[]{:S(2)}, u32[]{:S(2)}) collective-permute-start(bf16[128,128]{1,0:T(8,128)(2,1)S(1)} %fusion.2.refs_0_), channel_id=1, source_target_pairs={{0,4},{1,5},{2,6},{3,7},{4,0},{5,1},{6,2},{7,3},{8,12},{9,13},{10,... | collective-permute-start | bytes 98312 | tf_op jit(solution)/shard_map/ppermute | solution.py:24
  87.4 5.8 %collective-permute-start.28 = (bf16[128,128]{1,0:T(8,128)(2,1)S(1)}, bf16[128,128]{1,0:T(8,128)(2,1)S(1)}, u32[]{:S(2)}, u32[]{:S(2)}) collective-permute-start(bf16[128,128]{1,0:T(8,128)(2,1)S(1)} %fusion.2.refs_0_), channel_id=1, source_target_pairs={{0,6},{1,7},{2,4},{3,5},{4,2},{5,3},{6,0},{7,1},{8,14},{9,15},{10,... | collective-permute-start | bytes 98312 | tf_op jit(solution)/shard_map/ppermute | solution.py:24
  101.5 5.7 %collective-permute-start.32 = (bf16[128,128]{1,0:T(8,128)(2,1)S(1)}, bf16[128,128]{1,0:T(8,128)(2,1)S(1)}, u32[]{:S(2)}, u32[]{:S(2)}) collective-permute-start(bf16[128,128]{1,0:T(8,128)(2,1)S(1)} %fusion.1), channel_id=1, source_target_pairs={{0,2},{1,3},{2,0},{3,1},{4,6},{5,7},{6,4},{7,5},{8,10},{9,11},{10,... | collective-permute-start | bytes 98312 | tf_op jit(solution)/shard_map/ppermute | solution.py:24
  101.5 7.8 %collective-permute-start.33 = (bf16[128,128]{1,0:T(8,128)(2,1)S(1)}, bf16[128,128]{1,0:T(8,128)(2,1)S(1)}, u32[]{:S(2)}, u32[]{:S(2)}) collective-permute-start(bf16[128,128]{1,0:T(8,128)(2,1)S(1)} %fusion.1), channel_id=1, source_target_pairs={{0,4},{1,5},{2,6},{3,7},{4,0},{5,1},{6,2},{7,3},{8,12},{9,13},{10,... | collective-permute-start | bytes 98312 | tf_op jit(solution)/shard_map/ppermute | solution.py:24
  104.1 6.9 %collective-permute-start.34 = (bf16[128,128]{1,0:T(8,128)(2,1)S(1)}, bf16[128,128]{1,0:T(8,128)(2,1)S(1)}, u32[]{:S(2)}, u32[]{:S(2)}) collective-permute-start(bf16[128,128]{1,0:T(8,128)(2,1)S(1)} %fusion.1), channel_id=1, source_target_pairs={{0,6},{1,7},{2,4},{3,5},{4,2},{5,3},{6,0},{7,1},{8,14},{9,15},{10,... | collective-permute-start | bytes 98312 | tf_op jit(solution)/shard_map/ppermute | solution.py:24
  107.2 8.7 %collective-permute-start.59 = (bf16[2,64,512]{2,1,0:T(8,128)(2,1)S(1)}, bf16[2,64,512]{2,1,0:T(8,128)(2,1)S(1)}, u32[]{:S(2)}, u32[]{:S(2)}) collective-permute-start(bf16[2,64,512]{2,1,0:T(8,128)(2,1)S(1)} %get-tuple-element.155.refs_2_), channel_id=1, source_target_pairs={{0,6},{1,7},{2,4},{3,5},{4,2},{5,3},{6,0},{7,1},{8,14},{9,15},{10,... | collective-permute-start | bytes 393224 | tf_op jit(solution)/shard_map/ppermute | solution.py:24
  109.3 6.6 %collective-permute-start.60 = (bf16[4,64,512]{2,1,0:T(8,128)(2,1)S(1)}, bf16[4,64,512]{2,1,0:T(8,128)(2,1)S(1)}, u32[]{:S(2)}, u32[]{:S(2)}) collective-permute-start(bf16[4,64,512]{2,1,0:T(8,128)(2,1)S(1)} %get-tuple-element.153.refs_0_), channel_id=1, source_target_pairs={{0,8},{8,0},{16,24},{24,16},{1,9},{9,1},{17,25},{25,17},{2,10},{10... | collective-permute-start | bytes 786440 | tf_op jit(solution)/shard_map/ppermute | solution.py:24
  125.6 37.9 %collective-permute-start.61 = (bf16[4,2,64,512]{3,2,1,0:T(8,128)(2,1)S(1)}, bf16[4,2,64,512]{3,2,1,0:T(8,128)(2,1)S(1)}, u32[]{:S(2)}, u32[]{:S(2)}) collective-permute-start(bf16[4,2,64,512]{3,2,1,0:T(8,128)(2,1)S(1)} %pad_maximum_fusion), channel_id=1, source_target_pairs={{0,1},{1,0},{2,3},{3,2},{4,5},{5,4},{6,7},{7,6},{8,9},{9,8},{10,11... | collective-permute-start | bytes 1572872 | tf_op jit(solution)/shard_map/ppermute | solution.py:24
  129.0 6.3 %collective-permute-start.42 = (bf16[1,128,128]{2,1,0:T(8,128)(2,1)S(1)}, bf16[1,128,128]{2,1,0:T(8,128)(2,1)S(1)}, u32[]{:S(2)}, u32[]{:S(2)}) collective-permute-start(bf16[1,128,128]{2,1,0:T(8,128)(2,1)S(1)} %fusion.11.refs_0_), channel_id=1, source_target_pairs={{0,8},{8,0},{16,24},{24,16},{1,9},{9,1},{17,25},{25,17},{2,10},{10... | collective-permute-start | bytes 98312 | tf_op jit(solution)/shard_map/ppermute | solution.py:24
  142.3 18.0 %collective-permute-start.35 = (bf16[6,64,128]{2,1,0:T(8,128)(2,1)S(1)}, bf16[6,64,128]{2,1,0:T(8,128)(2,1)S(1)}, u32[]{:S(2)}, u32[]{:S(2)}) collective-permute-start(bf16[6,64,128]{2,1,0:T(8,128)(2,1)S(1)} %constant_dynamic-update-slice_fusion.6), channel_id=1, source_target_pairs={{0,1},{1,0},{2,3},{3,2},{4,5},{5,4},{6,7},{7,6},{8,9},{9,8},{10,11... | collective-permute-start | bytes 294920 | tf_op jit(solution)/shard_map/ppermute | solution.py:24
  147.0 6.4 %collective-permute-start.48 = (bf16[1,128,128]{2,1,0:T(8,128)(2,1)S(1)}, bf16[1,128,128]{2,1,0:T(8,128)(2,1)S(1)}, u32[]{:S(2)}, u32[]{:S(2)}) collective-permute-start(bf16[1,128,128]{2,1,0:T(8,128)(2,1)S(1)} %fusion.12.refs_0_), channel_id=1, source_target_pairs={{0,8},{8,0},{16,24},{24,16},{1,9},{9,1},{17,25},{25,17},{2,10},{10... | collective-permute-start | bytes 98312 | tf_op jit(solution)/shard_map/ppermute | solution.py:24
  147.7 5.7 %collective-permute-start.49 = (bf16[1,128,128]{2,1,0:T(8,128)(2,1)S(1)}, bf16[1,128,128]{2,1,0:T(8,128)(2,1)S(1)}, u32[]{:S(2)}, u32[]{:S(2)}) collective-permute-start(bf16[1,128,128]{2,1,0:T(8,128)(2,1)S(1)} %fusion.12.refs_0_), channel_id=1, source_target_pairs={{0,16},{8,24},{16,0},{24,8},{1,17},{9,25},{17,1},{25,9},{2,18},{10... | collective-permute-start | bytes 98312 | tf_op jit(solution)/shard_map/ppermute | solution.py:24
  155.8 8.9 %collective-permute-start.51 = (bf16[2,128,128]{2,1,0:T(8,128)(2,1)S(1)}, bf16[2,128,128]{2,1,0:T(8,128)(2,1)S(1)}, u32[]{:S(2)}, u32[]{:S(2)}) collective-permute-start(bf16[2,128,128]{2,1,0:T(8,128)(2,1)S(1)} %get-tuple-element.147), channel_id=1, source_target_pairs={{0,2},{1,3},{2,0},{3,1},{4,6},{5,7},{6,4},{7,5},{8,10},{9,11},{10,... | collective-permute-start | bytes 196616 | tf_op jit(solution)/shard_map/ppermute | solution.py:24
  155.9 8.8 %collective-permute-start.52 = (bf16[2,128,128]{2,1,0:T(8,128)(2,1)S(1)}, bf16[2,128,128]{2,1,0:T(8,128)(2,1)S(1)}, u32[]{:S(2)}, u32[]{:S(2)}) collective-permute-start(bf16[2,128,128]{2,1,0:T(8,128)(2,1)S(1)} %get-tuple-element.148), channel_id=1, source_target_pairs={{0,4},{1,5},{2,6},{3,7},{4,0},{5,1},{6,2},{7,3},{8,12},{9,13},{10,... | collective-permute-start | bytes 196616 | tf_op jit(solution)/shard_map/ppermute | solution.py:24
  158.0 6.8 %collective-permute-start.53 = (bf16[2,128,128]{2,1,0:T(8,128)(2,1)S(1)}, bf16[2,128,128]{2,1,0:T(8,128)(2,1)S(1)}, u32[]{:S(2)}, u32[]{:S(2)}) collective-permute-start(bf16[2,128,128]{2,1,0:T(8,128)(2,1)S(1)} %get-tuple-element.149), channel_id=1, source_target_pairs={{0,6},{1,7},{2,4},{3,5},{4,2},{5,3},{6,0},{7,1},{8,14},{9,15},{10,... | collective-permute-start | bytes 196616 | tf_op jit(solution)/shard_map/ppermute | solution.py:24
  164.7 7.3 %collective-permute-start.62 = (bf16[4,64,512]{2,1,0:T(8,128)(2,1)S(1)}, bf16[4,64,512]{2,1,0:T(8,128)(2,1)S(1)}, u32[]{:S(2)}, u32[]{:S(2)}) collective-permute-start(bf16[4,64,512]{2,1,0:T(8,128)(2,1)S(1)} %shard_map.82.refs_6_), channel_id=1, source_target_pairs={{0,1},{1,0},{2,3},{3,2},{4,5},{5,4},{6,7},{7,6},{8,9},{9,8},{10,11... | collective-permute-start | bytes 786440 | tf_op jit(solution)/shard_map/ppermute | solution.py:24
  174.3 6.8 %collective-permute-start.64 = (bf16[2,128,128]{2,1,0:T(8,128)(2,1)S(1)}, bf16[2,128,128]{2,1,0:T(8,128)(2,1)S(1)}, u32[]{:S(2)}, u32[]{:S(2)}) collective-permute-start(bf16[2,128,128]{2,1,0:T(8,128)(2,1)S(1)} %get-tuple-element.162), channel_id=1, source_target_pairs={{0,4},{1,5},{2,6},{3,7},{4,0},{5,1},{6,2},{7,3},{8,12},{9,13},{10,... | collective-permute-start | bytes 196616 | tf_op jit(solution)/shard_map/ppermute | solution.py:24
  176.6 6.1 %collective-permute-start.65 = (bf16[2,128,128]{2,1,0:T(8,128)(2,1)S(1)}, bf16[2,128,128]{2,1,0:T(8,128)(2,1)S(1)}, u32[]{:S(2)}, u32[]{:S(2)}) collective-permute-start(bf16[2,128,128]{2,1,0:T(8,128)(2,1)S(1)} %get-tuple-element.163), channel_id=1, source_target_pairs={{0,6},{1,7},{2,4},{3,5},{4,2},{5,3},{6,0},{7,1},{8,14},{9,15},{10,... | collective-permute-start | bytes 196616 | tf_op jit(solution)/shard_map/ppermute | solution.py:24
  (40 other events, 198.9 us)

commit v2 on v1

--- a/solution.py
+++ b/solution.py
@@ -9,7 +9,7 @@
 F32 = jnp.float32
 BF16 = jnp.bfloat16
 VMEM_LIMIT = 16 * 2**20
-SKIP_LEVEL = 4
+CUTS = 2
 
 
 def chip_order(count):
@@ -111,7 +111,28 @@
     return call(body, outs + (held if keep else []), scalars, arrays, scratch, far=2)
 
 
-def skip_level(scalars, upper, lower_mine, lower_theirs, folded, at):
+def fold_more(scalars, own, inverses, spans):
+    _, half, full = own.shape
+    total = sum(count for _, _, count in spans)
+    used = sorted({level for level, _, _ in spans})
+
+    def body(s, w, own_ref, inv_ref, out_ref, folded_ref):
+        for i, level in enumerate(used):
+            folded_ref[i] = masked_inverse(inv_ref[level], s[3 + level])
+        cursor = 0
+        for level, at, count in spans:
+            flat = own_ref[pl.ds(at, count)].reshape(count * half, full)
+            product = dot(flat, folded_ref[used.index(level)]).reshape(count, half, full)
+            for p in range(count):
+                out_ref[cursor + p] = (product[p] * w[at + p].astype(F32)).astype(BF16)
+            cursor += count
+
+    outs = [((total, half, full), BF16)]
+    scratch = [pltpu.VMEM((len(used), full, full), BF16)]
+    return call(body, outs, scalars, [own, inverses], scratch)
+
+
+def skip_level(scalars, upper, lower_mine, lower_theirs, direct, at):
     count, half, full = upper[0].shape
     n, chips = len(upper), len(lower_mine)
 
@@ -131,7 +152,7 @@
         out_ref[...] = (direct - total.reshape(count, half, full)).astype(BF16)
 
     outs = [((count, half, full), BF16)]
-    arrays = [*upper, *lower_mine, lower_theirs, folded]
+    arrays = [*upper, *lower_mine, lower_theirs, direct]
     return call(body, outs, scalars[:1], arrays, [pltpu.VMEM((n, full, full), BF16)])
 
 
@@ -273,19 +294,22 @@
     n_p = len(pieces)
     sums = [o[2] for o in outputs if o[2] is not None]
     tall = max(len(v) for v in vectors) * half
+    n_terms = sum(len(terms) for _, terms, _, _ in outputs)
 
     def body(s, w, *refs):
         piece_refs, side_refs, inv_ref = refs[:n_p], refs[n_p : n_p + 2], refs[n_p + 2]
         waiting = list(refs[n_p + 3 : n_p + 3 + len(sums)])
         outs, stack_ref = refs[n_p + 3 + len(sums) : -1], refs[-1]
         core, leaf = s[1], s[2]
+        place = 0
         for slot, (level, terms, total, complete) in enumerate(outputs):
             now = None if total is None else waiting.pop(0)[...]
             for v, at in terms:
                 count = len(vectors[v])
                 lefts = two_sides(
-                    stack_ref.at[slot], piece_refs, vectors[v], leaf, core, (w, at)
+                    stack_ref.at[place], piece_refs, vectors[v], leaf, core, (w, at)
                 )
+                place += 1
                 for side in range(2):
                     flat = side_refs[side][pl.ds(at, count)].reshape(count * half, full)
                     product = dot(lefts[side], flat)
@@ -298,7 +322,7 @@
 
     outs = [((columns, full), F32)] * len(outputs)
     arrays = [*pieces, *sides, inverses, *sums]
-    return call(body, outs, scalars, arrays, [pltpu.VMEM((len(outputs), 2, tall, columns), BF16)])
+    return call(body, outs, scalars, arrays, [pltpu.VMEM((n_terms, 2, tall, columns), BF16)])
 
 
 def shards(rhs, diag_inverse, factor, widths, structure):
@@ -312,7 +336,7 @@
     first = core == 0
     offsets = block_offsets(levels, leaf_count)
     group = [group_size(l, leaf_count) for l in range(levels)]
-    top = levels - 1
+    top, mid, low = levels - 1, levels - 2, levels - 3
 
     def in_order(mine, theirs, axis):
         return jnp.where(
@@ -344,40 +368,54 @@
 
     folded_at = {}
 
-    def fold(pairs, picked, blocks, levels, keep):
+    def spans_of(pairs):
         cursor, spans = 0, []
         for s, t in pairs:
             folded_at[s, t] = cursor
             spans.append((s, offsets[s, t], group[t]))
             cursor += group[t]
-        mine, half, *held = fold_blocks(
-            scalars,
-            factor[0],
-            diag_inverse[0],
-            spans,
-            [pairs.index(picked)],
-            blocks,
-            levels,
-            keep,
-        )
-        theirs = from_partner(mine, "row", 1)
-        return (mine, theirs), half, held
+        return spans
+
+    def swap(mine):
+        return mine, from_partner(mine, "row", 1)
+
+    def fold(pairs, picked, blocks, levels, keep):
+        places = [pairs.index(pair) for pair in picked]
+        mine, *others = fold_blocks(scalars, factor[0], diag_inverse[0], spans_of(pairs), places, blocks, levels, keep)
+        return swap(mine), others[: len(picked)], others[len(picked) :]
 
     lowest = [(0, 1), (0, 2)]
-    folded_first, lower_half, _ = fold(lowest, (0, 1), group[1] + group[2], 1, False)
-    others = sorted([(s, s + 1) for s in range(1, top)] + [(1, 3)])
-    folded, upper_half, (own_blocks, inverses) = fold(others, (1, 2), factor.shape[1], levels, True)
+    folded_first, (lower_half,), _ = fold(lowest, [(0, 1)], group[1] + group[2], 1, False)
+    others = [(s, s + 1) for s in range(1, top)]
+    folded, (upper_half, high_lower, high_upper), (own_blocks, inverses) = fold(
+        others, [(1, 2), (low, mid), (mid, top)], factor.shape[1], levels, True
+    )
+    late = sorted([(s, t) for s in range(1, low) for t in (low, mid) if t > s + 1] + [(low, top)])
+    (late_mine,) = fold_more(scalars, own_blocks, inverses, spans_of(late))
+    folded_late = swap(late_mine)
     their_blocks = from_partner(factor[0], "row", 1)
     sides = [own_blocks, their_blocks]
-    lower_mine = gather_chips(lower_half)
+
+    def spread(piece, cuts):
+        gathered = [piece]
+        for k in range(1, chips):
+            count = piece.shape[0] // cuts[k]
+            got = []
+            for i in range(cuts[k]):
+                got.append(from_partner(piece[i * count : (i + 1) * count], "row", 2 * k))
+            gathered.append(got[0] if len(got) == 1 else jnp.concatenate(got))
+        return gathered
+
+    lower_mine = spread(lower_half, cuts_of(chips, 1))
     upper = [upper_half] + exchange_leaves([upper_half] * (group[1] - 1))
-
-    def skip_product(lower_mine, upper, after):
-        lower_mine, upper, _ = lax.optimization_barrier((lower_mine, upper, after))
+    high_mine = spread(high_lower, cuts_of(chips, CUTS))
+    high = [high_upper] + exchange_leaves([high_upper] * (leaf_count - 1))
+
+    def skip_product(upper, lower_mine, direct, at, after):
+        upper, lower_mine, _ = lax.optimization_barrier((upper, lower_mine, after))
         lower_theirs = from_partner(jnp.stack(lower_mine), "row", 1)
-        (mine,) = skip_level(scalars, upper, lower_mine, lower_theirs, folded_first[0], folded_at[0, 2])
-        theirs = from_partner(mine, "row", 1)
-        return mine, theirs
+        (mine,) = skip_level(scalars, upper, lower_mine, lower_theirs, direct, at)
+        return swap(mine)
 
     pending = {t: None for t in range(levels)}
     turned, kept, sent = [None] * levels, [None] * levels, [None] * levels
@@ -407,8 +445,7 @@
         parts = gather_chips(now)
         if l < top:
             own, *messages = push_level(l, parts)
-        if l == SKIP_LEVEL:
-            skip = skip_product(lower_mine, upper, own)
+    high_skip = skip_product(high, high_mine, late_mine, folded_at[low, top], own)
     finish_level(top, parts)
 
     adjoint = [None] * levels
@@ -430,24 +467,41 @@
         return total
 
     adjoint[top] = turned[top].astype(BF16)
-    pieces, vectors = gather_leaves([(top, adjoint[top])])
-    sums = {s: None for s in range(levels)}
-    for l in range(top - 1, 1, -1):
-        t = l + 1
-        outputs = [([(0, 0, folded_at[l, t])], sums[l])]
+    pieces, vectors = gather_leaves([(top, adjoint[top]), (mid, turned[mid].astype(BF16))])
+    outputs = [
+        ([(0, 1, 0), (1, 0, folded_at[low, mid])], None),
+        ([(0, 0, folded_at[mid, top])], None),
+    ]
+    own, *messages = pull(scalars, pieces, vectors, outputs, [folded, high_skip], full, chips)
+    received = exchange_chips(messages)
+    listed = [(s, [(0, offsets[s, top])], None, s > 0) for s in range(low)]
+    sums = dict(enumerate(pull_rest(scalars, pieces, vectors[:1], listed, sides, inverses)))
+    adjoint[low] = (turned[low] - total_of(own, received, 0)).astype(BF16)
+    adjoint[mid] = (turned[mid] - total_of(own, received, 1)).astype(BF16)
+    uppers = [low, mid]
+    pieces, vectors = gather_leaves([(t, adjoint[t]) for t in uppers])
+    for l in range(low - 1, 1, -1):
+
+        def term(s, i, t):
+            return (i, 0, folded_at[s, t]) if t == s + 1 else (i, 1, folded_at[s, t])
+
+        lower = [l, 1] if l == 2 else [l]
+        outputs = [([term(s, i, t) for i, t in enumerate(uppers)], sums[s]) for s in lower]
+        own, *messages = pull(scalars, pieces, vectors, outputs, [folded, folded_late], full, chips)
+        received = exchange_chips(messages)
         if l == 2:
-            outputs.append(([(0, 0, folded_at[1, t])], sums[1]))
-        own, *messages = pull(scalars, pieces, vectors, outputs, [folded], full, chips)
-        received = exchange_chips(messages)
-        sources = [s for s in range(t - 1) if (s, t) != (1, 3)]
-        complete = {t - 2} if t > 4 else {1, 2} if t == 4 else {0}
-        listed = [(s, [(0, offsets[s, t])], sums[s], s in complete) for s in sources]
-        sums.update(zip(sources, pull_rest(scalars, pieces, vectors, listed, sides, inverses)))
+            skip = skip_product(upper, lower_mine, folded_first[0], folded_at[0, 2], own)
+        left = [s for s in range(l) if s not in lower]
+        listed = [
+            (s, [(i, offsets[s, t]) for i, t in enumerate(uppers)], sums[s], l == 2) for s in left
+        ]
+        sums.update(zip(left, pull_rest(scalars, pieces, vectors, listed, sides, inverses)))
         adjoint[l] = (turned[l] - total_of(own, received, 0)).astype(BF16)
         named = [(l, adjoint[l])]
         if l == 2:
             ahead = turned[1] - total_of(own, received, 1)
             named.append((1, ahead.astype(BF16)))
+        uppers = [l]
         pieces, vectors = gather_leaves(named)
     outputs = [
         ([(0, 1, 0), (1, 2, folded_at[0, 1])], sums[0]),
@@ -470,6 +524,10 @@
     upper_levels = swap_rows(adjoint[2:])
     backward = jnp.concatenate([swap_rows(adjoint[:2]), upper_levels])
     return forward[:, None], backward[:, None]
+
+
+def cuts_of(chips, most):
+    return [most if k >= chips // 2 else 1 for k in range(chips)]
 
 
 def solution(mesh):

time: 185 us -> 193 us (1.043)
  starting transfers between devices: 86.6 us -> 91.8 us
  waiting for transfers between devices: 40.5 us -> 44 us
    ppermute x68 -> x73, starting transfers between devices: 86.6 us -> 91.8 us  [from_partner(): lax.ppermute(x, axis, [(i, i ^ mask) for i in range(lax.axis_size(axis))])]
    ppermute x68 -> x73, waiting for transfers between devices: 40.5 us -> 44 us  [from_partner(): lax.ppermute(x, axis, [(i, i ^ mask) for i in range(lax.axis_size(axis))])]
    pallas_call x17 -> x18, Pallas kernels: 41.6 us -> 39.9 us  [call(): pl.pallas_call(body, out_shape=[jax.ShapeDtypeStruct(s, d) for s, d in ou...]
    unnamed x15 -> x24, local copies, waits for them, and re-layouts: 2.61 us -> 3.98 us
    pallas_call x4 -> x3, local copies, waits for them, and re-layouts: 8.6 us -> 7.59 us  [call(): pl.pallas_call(body, out_shape=[jax.ShapeDtypeStruct(s, d) for s, d in ou...]
  transfers between devices with their start and end apart: 68 -> 73, of which waited for: 31 -> 30; matrix products, arithmetic and copies ran while one was open for 6% -> 5% of each run, Pallas kernels for 17% -> 17%
where the time goes in v2:
time: 193 us; the launch traced here: 192 us
  starting transfers between devices  91.8 us (48%)
  waiting for transfers between devices  44 us (23%)
  Pallas kernels  39.9 us (21%)
  local copies, waits for them, and re-layouts  11.6 us (6%)
  other arithmetic  3.83 us (2%)
    ppermute x73, starting transfers between devices, from_partner(): lax.ppermute(x, axis, [(i, i ^ mask) for i in range(lax.axis_size(axis))])  91.8 us
    ppermute x73, waiting for transfers between devices, from_partner(): lax.ppermute(x, axis, [(i, i ^ mask) for i in range(lax.axis_size(axis))])  44 us
    pallas_call x18, Pallas kernels, call(): pl.pallas_call(body, out_shape=[jax.ShapeDtypeStruct(s, d) for s, d in ou...  39.9 us
    pallas_call x3, local copies, waits for them, and re-layouts, call(): pl.pallas_call(body, out_shape=[jax.ShapeDtypeStruct(s, d) for s, d in ou...  7.59 us
    unnamed x24, local copies, waits for them, and re-layouts  3.98 us
  transfers between devices with their start and end apart: 73, of which 30 were waited for; matrix products, arithmetic and copies ran while one was open for 5% of the time, Pallas kernels for 17%

profile of v2, /device:TPU:0, one launch (start us, length us, event | category | flops | bytes accessed | tf_op | source)
XLA Modules:
  0.0 192.3 jit_solution(1308274431820931185)
XLA Ops:
  2.6 5.5 %shard_map.68 = (bf16[16,64,512]{2,1,0:T(8,128)(2,1)}, bf16[4,64,512]{2,1,0:T(8,128)(2,1)S(1)}, bf16[4,64,512]{2,1,0:T(8,128)(2,1)S(1)}, bf16[4,64,512]{2,1,0:T(...) custom-call(s32[9]{0:T(128)S(1)} %pad_add_fusion.s, s32[58]{0:T(128)S(1)} %bitcast.136, ...), custom_call_target="tpu_custom_call" | custom-call | tf_op jit(solution)/shard_map/pallas_call | solution.py:48
  12.9 2.3 %shard_map.70 = (bf16[6,64,512]{2,1,0:T(8,128)(2,1)S(1)}, bf16[2,64,512]{2,1,0:T(8,128)(2,1)S(1)}) custom-call(s32[9]{0:T(128)S(1)} %pad_add_fusion.s, s32[58]{0:T(128)S(1)} %bitcast.137, bf16[58,64,512]{2,1,0:T(8,128)(2,1)} %bitcast.149, bf16[6,512,512]{2,1,0:T(8,128)(2,1)} %bitcast.151), custom_call_target="tpu_custom_call" | custom-call | tf_op jit(solution)/shard_map/pallas_call | solution.py:48
  15.7 2.8 %collective-permute-start.1 = (bf16[128,128]{1,0:T(8,128)(2,1)S(1)}, bf16[128,128]{1,0:T(8,128)(2,1)S(1)}, u32[]{:S(2)}, u32[]{:S(2)}) collective-permute-start(bf16[128,128]{1,0:T(8,128)(2,1)S(1)} %slice_bitcast_fusion.5.refs_0_), channel_id=1, source_target_pairs={{0,2},{1,3},{2,0},{3,1},{4,6},{5,7},{6,4},{7,5},{8,10},{9,11},{10,... | collective-permute-start | bytes 98312 | tf_op jit(solution)/shard_map/ppermute | solution.py:24
  18.5 2.6 %collective-permute-start.2 = (bf16[128,128]{1,0:T(8,128)(2,1)S(1)}, bf16[128,128]{1,0:T(8,128)(2,1)S(1)}, u32[]{:S(2)}, u32[]{:S(2)}) collective-permute-start(bf16[128,128]{1,0:T(8,128)(2,1)S(1)} %slice_bitcast_fusion.5.refs_0_), channel_id=1, source_target_pairs={{0,4},{1,5},{2,6},{3,7},{4,0},{5,1},{6,2},{7,3},{8,12},{9,13},{10,... | collective-permute-start | bytes 98312 | tf_op jit(solution)/shard_map/ppermute | solution.py:24
  21.1 3.3 %collective-permute-start.3 = (bf16[128,128]{1,0:T(8,128)(2,1)S(1)}, bf16[128,128]{1,0:T(8,128)(2,1)S(1)}, u32[]{:S(2)}, u32[]{:S(2)}) collective-permute-start(bf16[128,128]{1,0:T(8,128)(2,1)S(1)} %slice_bitcast_fusion.5.refs_0_), channel_id=1, source_target_pairs={{0,6},{1,7},{2,4},{3,5},{4,2},{5,3},{6,0},{7,1},{8,14},{9,15},{10,... | collective-permute-start | bytes 98312 | tf_op jit(solution)/shard_map/ppermute | solution.py:24
  24.4 2.4 %collective-permute-done.3.refs_3_ = bf16[128,128]{1,0:T(8,128)(2,1)S(1)} collective-permute-done((bf16[128,128]{1,0:T(8,128)(2,1)S(1)}, bf16[128,128]{1,0:T(8,128)(2,1)S(1)}, u32[]{:S(2)}, u32[]{:S(2)}) %collective-permute-start.3) | collective-permute-done | bytes 32800 | tf_op jit(solution)/shard_map/ppermute | solution.py:24
  29.2 2.4 %collective-permute-done.6 = bf16[128,128]{1,0:T(8,128)(2,1)S(1)} collective-permute-done((bf16[128,128]{1,0:T(8,128)(2,1)S(1)}, bf16[128,128]{1,0:T(8,128)(2,1)S(1)}, u32[]{:S(2)}, u32[]{:S(2)}) %collective-permute-start.6) | collective-permute-done | bytes 32800 | tf_op jit(solution)/shard_map/ppermute | solution.py:24
  31.7 3.9 %collective-permute-start.8 = (bf16[128,128]{1,0:T(8,128)(2,1)S(1)}, bf16[128,128]{1,0:T(8,128)(2,1)S(1)}, u32[]{:S(2)}, u32[]{:S(2)}) collective-permute-start(bf16[128,128]{1,0:T(8,128)(2,1)S(1)} %fusion.5.refs_0_), channel_id=1, source_target_pairs={{0,4},{1,5},{2,6},{3,7},{4,0},{5,1},{6,2},{7,3},{8,12},{9,13},{10,... | collective-permute-start | bytes 98312 | tf_op jit(solution)/shard_map/ppermute | solution.py:24
  36.1 3.4 %shard_map.69 = (f32[128,128]{1,0:T(8,128)S(1)}, bf16[64,128]{1,0:T(8,128)(2,1)S(1)}, bf16[64,128]{1,0:T(8,128)(2,1)S(1)}, f32[4,128,128]{2,1,0:T(8,128)S(1)}, f...) custom-call(s32[9]{0:T(128)S(1)} %pad_add_fusion.s, s32[58]{0:T(128)S(1)} %bitcast.138, ...), custom_call_target="tpu_custom_call" | custom-call | tf_op jit(solution)/shard_map/pallas_call | solution.py:48
  43.2 2.5 %collective-permute-start.13 = (bf16[128,128]{1,0:T(8,128)(2,1)S(1)}, bf16[128,128]{1,0:T(8,128)(2,1)S(1)}, u32[]{:S(2)}, u32[]{:S(2)}) collective-permute-start(bf16[128,128]{1,0:T(8,128)(2,1)S(1)} %get-tuple-element.100), channel_id=1, source_target_pairs={{0,24},{8,16},{16,8},{24,0},{1,25},{9,17},{17,9},{25,1},{2,26},{10... | collective-permute-start | bytes 98312 | tf_op jit(solution)/shard_map/ppermute | solution.py:24
  52.3 2.3 %collective-permute-start.16 = (bf16[128,128]{1,0:T(8,128)(2,1)S(1)}, bf16[128,128]{1,0:T(8,128)(2,1)S(1)}, u32[]{:S(2)}, u32[]{:S(2)}) collective-permute-start(bf16[128,128]{1,0:T(8,128)(2,1)S(1)} %fusion.4.refs_0_), channel_id=1, source_target_pairs={{0,6},{1,7},{2,4},{3,5},{4,2},{5,3},{6,0},{7,1},{8,14},{9,15},{10,... | collective-permute-start | bytes 98312 | tf_op jit(solution)/shard_map/ppermute | solution.py:24
  54.6 3.3 %shard_map.72 = (f32[128,128]{1,0:T(8,128)S(1)}, bf16[64,128]{1,0:T(8,128)(2,1)S(1)}, bf16[64,128]{1,0:T(8,128)(2,1)S(1)}, f32[4,128,128]{2,1,0:T(8,128)S(1)}, f...) custom-call(s32[9]{0:T(128)S(1)} %pad_add_fusion.s, s32[58]{0:T(128)S(1)} %bitcast.139, ...), custom_call_target="tpu_custom_call" | custom-call | tf_op jit(solution)/shard_map/pallas_call | solution.py:48
  66.0 2.8 %collective-permute-start.21 = (bf16[128,128]{1,0:T(8,128)(2,1)S(1)}, bf16[128,128]{1,0:T(8,128)(2,1)S(1)}, u32[]{:S(2)}, u32[]{:S(2)}) collective-permute-start(bf16[128,128]{1,0:T(8,128)(2,1)S(1)} %fusion.3.refs_0_), channel_id=1, source_target_pairs={{0,4},{1,5},{2,6},{3,7},{4,0},{5,1},{6,2},{7,3},{8,12},{9,13},{10,... | collective-permute-start | bytes 98312 | tf_op jit(solution)/shard_map/ppermute | solution.py:24
  70.4 3.2 %shard_map.88 = (bf16[6,64,128]{2,1,0:T(8,128)(2,1)S(1)}, f32[4,128,128]{2,1,0:T(8,128)S(1)}, f32[4,128,128]{2,1,0:T(8,128)S(1)}, bf16[64,128]{1,0:T(8,128)(2,1)S(1)}, f32[128,128]{1,0:T(8,128)S(1)}) fusion(bf16[6,64,128]{2,1,0:T(8,128)(2,1)S(1)} %constant_dynamic-update-slice_fusion.4, s32[9]{0:T(128)S(1)} %pad_add_fusion.s, s32[58]{0:T(128)S(1)} %bitcast.140, ...), kind=kCustom, calls=%fused_computation.62 | custom fusion | bytes 12026880 | tf_op jit(solution)/shard_map/pallas_call | solution.py:48
  76.8 2.5 %collective-permute-start.25 = (bf16[128,128]{1,0:T(8,128)(2,1)S(1)}, bf16[128,128]{1,0:T(8,128)(2,1)S(1)}, u32[]{:S(2)}, u32[]{:S(2)}) collective-permute-start(bf16[128,128]{1,0:T(8,128)(2,1)S(1)} %get-tuple-element.115), channel_id=1, source_target_pairs={{0,24},{8,16},{16,8},{24,0},{1,25},{9,17},{17,9},{25,1},{2,26},{10... | collective-permute-start | bytes 98312 | tf_op jit(solution)/shard_map/ppermute | solution.py:24
  80.4 4.6 %collective-permute-start.44 = (bf16[2,64,512]{2,1,0:T(8,128)(2,1)S(1)}, bf16[2,64,512]{2,1,0:T(8,128)(2,1)S(1)}, u32[]{:S(2)}, u32[]{:S(2)}) collective-permute-start(bf16[2,64,512]{2,1,0:T(8,128)(2,1)S(1)} %get-tuple-element.202), channel_id=1, source_target_pairs={{0,4},{1,5},{2,6},{3,7},{4,0},{5,1},{6,2},{7,3},{8,12},{9,13},{10,... | collective-permute-start | bytes 393224 | tf_op jit(solution)/shard_map/ppermute | solution.py:24
  85.0 2.2 %collective-permute-start.46 = (bf16[2,64,512]{2,1,0:T(8,128)(2,1)S(1)}, bf16[2,64,512]{2,1,0:T(8,128)(2,1)S(1)}, u32[]{:S(2)}, u32[]{:S(2)}) collective-permute-start(bf16[2,64,512]{2,1,0:T(8,128)(2,1)S(1)} %get-tuple-element.202), channel_id=1, source_target_pairs={{0,6},{1,7},{2,4},{3,5},{4,2},{5,3},{6,0},{7,1},{8,14},{9,15},{10,... | collective-permute-start | bytes 393224 | tf_op jit(solution)/shard_map/ppermute | solution.py:24
  88.9 2.3 %collective-permute-start.26 = (bf16[128,128]{1,0:T(8,128)(2,1)S(1)}, bf16[128,128]{1,0:T(8,128)(2,1)S(1)}, u32[]{:S(2)}, u32[]{:S(2)}) collective-permute-start(bf16[128,128]{1,0:T(8,128)(2,1)S(1)} %fusion.2.refs_0_), channel_id=1, source_target_pairs={{0,2},{1,3},{2,0},{3,1},{4,6},{5,7},{6,4},{7,5},{8,10},{9,11},{10,... | collective-permute-start | bytes 98312 | tf_op jit(solution)/shard_map/ppermute | solution.py:24
  92.4 5.9 %collective-permute-done.43 = bf16[2,64,512]{2,1,0:T(8,128)(2,1)S(1)} collective-permute-done((bf16[2,64,512]{2,1,0:T(8,128)(2,1)S(1)}, bf16[2,64,512]{2,1,0:T(8,128)(2,1)S(1)}, u32[]{:S(2)}, u32[]{:S(2)}) %collective-permute-start.43) | collective-permute-done | bytes 131104 | tf_op jit(solution)/shard_map/ppermute | solution.py:24
  100.8 2.8 %collective-permute-start.27 = (bf16[128,128]{1,0:T(8,128)(2,1)S(1)}, bf16[128,128]{1,0:T(8,128)(2,1)S(1)}, u32[]{:S(2)}, u32[]{:S(2)}) collective-permute-start(bf16[128,128]{1,0:T(8,128)(2,1)S(1)} %fusion.2.refs_0_), channel_id=1, source_target_pairs={{0,4},{1,5},{2,6},{3,7},{4,0},{5,1},{6,2},{7,3},{8,12},{9,13},{10,... | collective-permute-start | bytes 98312 | tf_op jit(solution)/shard_map/ppermute | solution.py:24
  103.7 2.2 %collective-permute-done.27.refs_2_ = bf16[128,128]{1,0:T(8,128)(2,1)S(1)} collective-permute-done((bf16[128,128]{1,0:T(8,128)(2,1)S(1)}, bf16[128,128]{1,0:T(8,128)(2,1)S(1)}, u32[]{:S(2)}, u32[]{:S(2)}) %collective-permute-start.27) | collective-permute-done | bytes 32800 | tf_op jit(solution)/shard_map/ppermute | solution.py:24
  105.8 2.2 %collective-permute-start.28 = (bf16[128,128]{1,0:T(8,128)(2,1)S(1)}, bf16[128,128]{1,0:T(8,128)(2,1)S(1)}, u32[]{:S(2)}, u32[]{:S(2)}) collective-permute-start(bf16[128,128]{1,0:T(8,128)(2,1)S(1)} %fusion.2.refs_0_), channel_id=1, source_target_pairs={{0,6},{1,7},{2,4},{3,5},{4,2},{5,3},{6,0},{7,1},{8,14},{9,15},{10,... | collective-permute-start | bytes 98312 | tf_op jit(solution)/shard_map/ppermute | solution.py:24
  108.1 3.0 %shard_map.87 = (bf16[6,64,128]{2,1,0:T(8,128)(2,1)S(1)}, f32[4,128,128]{2,1,0:T(8,128)S(1)}, bf16[64,128]{1,0:T(8,128)(2,1)S(1)}, f32[128,128]{1,0:T(8,128)S(1)}) fusion(bf16[6,64,128]{2,1,0:T(8,128)(2,1)S(1)} %get-tuple-element.180, s32[9]{0:T(128)S(1)} %pad_add_fusion.s, s32[58]{0:T(128)S(1)} %bitcast.141, bf16[128,128]{1,0:T(8,128)(2,1)S(1)} %fusion.3.refs_0_, ...), kind=kCustom, calls=%fused_computation.61 | custom fusion | bytes 11502592 | tf_op jit(solution)/shard_map/pallas_call | solution.py:48
  124.7 2.2 %collective-permute-done.33 = bf16[128,128]{1,0:T(8,128)(2,1)S(1)} collective-permute-done((bf16[128,128]{1,0:T(8,128)(2,1)S(1)}, bf16[128,128]{1,0:T(8,128)(2,1)S(1)}, u32[]{:S(2)}, u32[]{:S(2)}) %collective-permute-start.33) | collective-permute-done | bytes 32800 | tf_op jit(solution)/shard_map/ppermute | solution.py:24
  137.2 2.2 %collective-permute-done.38.refs_3_ = bf16[2,128,128]{2,1,0:T(8,128)(2,1)S(1)} collective-permute-done((bf16[2,128,128]{2,1,0:T(8,128)(2,1)S(1)}, bf16[2,128,128]{2,1,0:T(8,128)(2,1)S(1)}, u32[]{:S(2)}, u32[]{:S(2)}) %collective-permute-start.38) | collective-permute-done | bytes 65568 | tf_op jit(solution)/shard_map/ppermute | solution.py:24
  143.2 2.8 %collective-permute-start.49 = (bf16[2,128,128]{2,1,0:T(8,128)(2,1)S(1)}, bf16[2,128,128]{2,1,0:T(8,128)(2,1)S(1)}, u32[]{:S(2)}, u32[]{:S(2)}) collective-permute-start(bf16[2,128,128]{2,1,0:T(8,128)(2,1)S(1)} %get-tuple-element.145), channel_id=1, source_target_pairs={{0,2},{1,3},{2,0},{3,1},{4,6},{5,7},{6,4},{7,5},{8,10},{9,11},{10,... | collective-permute-start | bytes 196616 | tf_op jit(solution)/shard_map/ppermute | solution.py:24
  157.0 2.9 %shard_map.81 = (f32[128,512]{1,0:T(8,128)S(1)}, f32[128,512]{1,0:T(8,128)S(1)}, f32[128,512]{1,0:T(8,128)S(1)}) custom-call(s32[9]{0:T(128)S(1)} %pad_add_fusion.s, s32[58]{0:T(128)S(1)} %bitcast.145, bf16[2,128,128]{2,1,0:T(8,128)(2,1)S(1)} %pad_maximum_fusion.5.refs_0_, bf16[2,128,128]{2,1,0:T(8,128)(2,1)S(1)} %collective-permute-done.36.refs_1_, ...), custom_call_target="tpu_custom_call" | custom-call | tf_op jit(solution)/shard_map/pallas_call | solution.py:48
  161.0 2.2 %shard_map.82 = (f32[2,128,128]{2,1,0:T(8,128)S(1)}, bf16[2,128,128]{2,1,0:T(8,128)(2,1)S(1)}, bf16[2,128,128]{2,1,0:T(8,128)(2,1)S(1)}, bf16[2,128,128]{2,1,0:T(8,128)(2,1)S(1)}) custom-call(s32[9]{0:T(128)S(1)} %pad_add_fusion.s, bf16[2,128,128]{2,1,0:T(8,128)(2,1)S(1)} %pad_maximum_fusion.6.refs_0_, ...), custom_call_target="tpu_custom_call" | custom-call | tf_op jit(solution)/shard_map/pallas_call | solution.py:48
  163.9 2.2 %collective-permute-start.58 = (bf16[2,128,128]{2,1,0:T(8,128)(2,1)S(1)}, bf16[2,128,128]{2,1,0:T(8,128)(2,1)S(1)}, u32[]{:S(2)}, u32[]{:S(2)}) collective-permute-start(bf16[2,128,128]{2,1,0:T(8,128)(2,1)S(1)} %get-tuple-element.153), channel_id=1, source_target_pairs={{0,6},{1,7},{2,4},{3,5},{4,2},{5,3},{6,0},{7,1},{8,14},{9,15},{10,... | collective-permute-start | bytes 196616 | tf_op jit(solution)/shard_map/ppermute | solution.py:24
  169.1 2.6 %shard_map.84.refs_10_ = f32[128,512]{1,0:T(8,128)S(1)} custom-call(s32[9]{0:T(128)S(1)} %pad_add_fusion.s, s32[58]{0:T(128)S(1)} %bitcast.146, bf16[2,128,128]{2,1,0:T(8,128)(2,1)S(1)} %pad_maximum_fusion.6.refs_0_, bf16[2,128,128]{2,1,0:T(8,128)(2,1)S(1)} %collective-permute-done.52.refs_1_, bf16[2,128,128]{2,1,0:T(8,128)(2,1)S(1)} %collective-permute-done.53.refs_2_, ...), custom_call_target="tpu_custom_call" | custom-call | tf_op jit(solution)/shard_map/pallas_call | solution.py:48
  184.2 2.4 %collective-permute-start.68 = (bf16[2,128,128]{2,1,0:T(8,128)(2,1)S(1)}, bf16[2,128,128]{2,1,0:T(8,128)(2,1)S(1)}, u32[]{:S(2)}, u32[]{:S(2)}) collective-permute-start(bf16[2,128,128]{2,1,0:T(8,128)(2,1)S(1)} %get-tuple-element.165), channel_id=1, source_target_pairs={{0,2},{1,3},{2,0},{3,1},{4,6},{5,7},{6,4},{7,5},{8,10},{9,11},{10,... | collective-permute-start | bytes 196616 | tf_op jit(solution)/shard_map/ppermute | solution.py:24
  186.7 2.3 %collective-permute-done.70 = bf16[2,128,128]{2,1,0:T(8,128)(2,1)S(1)} collective-permute-done((bf16[2,128,128]{2,1,0:T(8,128)(2,1)S(1)}, bf16[2,128,128]{2,1,0:T(8,128)(2,1)S(1)}, u32[]{:S(2)}, u32[]{:S(2)}) %collective-permute-start.70) | collective-permute-done | bytes 65568 | tf_op jit(solution)/shard_map/ppermute | solution.py:24
  (188 shorter events, 99.0 us)
Async XLA Ops:
  0.6 35.4 %collective-permute-start.4 = (bf16[58,64,512]{2,1,0:T(8,128)(2,1)}, bf16[58,64,512]{2,1,0:T(8,128)(2,1)}, u32[]{:S(2)}, u32[]{:S(2)}) collective-permute-start(bf16[58,64,512]{2,1,0:T(8,128)(2,1)} %bitcast.147), channel_id=1, source_target_pairs={{0,1},{1,0},{2,3},{3,2},{4,5},{5,4},{6,7},{7,6},{8,9},{9,8},{10,11... | collective-permute-start | bytes 11403272 | tf_op jit(solution)/shard_map/ppermute | solution.py:24
  11.3 30.0 %collective-permute-start.10 = (bf16[16,64,512]{2,1,0:T(8,128)(2,1)}, bf16[16,64,512]{2,1,0:T(8,128)(2,1)}, u32[]{:S(2)}, u32[]{:S(2)}) collective-permute-start(bf16[16,64,512]{2,1,0:T(8,128)(2,1)} %get-tuple-element.95.refs_4_), channel_id=1, source_target_pairs={{0,1},{1,0},{2,3},{3,2},{4,5},{5,4},{6,7},{7,6},{8,9},{9,8},{10,11... | collective-permute-start | bytes 3145736 | tf_op jit(solution)/shard_map/ppermute | solution.py:24
  15.2 11.6 %collective-permute-start.5 = (bf16[6,64,512]{2,1,0:T(8,128)(2,1)S(1)}, bf16[6,64,512]{2,1,0:T(8,128)(2,1)S(1)}, u32[]{:S(2)}, u32[]{:S(2)}) collective-permute-start(bf16[6,64,512]{2,1,0:T(8,128)(2,1)S(1)} %get-tuple-element.88.refs_4_.refs_7_.refs_8_), channel_id=1, source_target_pairs={{0,1},{1,0},{2,3},{3,2},{4,5},{5,4},{6,7},{7,6},{8,9},{9,8},{10,11... | collective-permute-start | bytes 1179656 | tf_op jit(solution)/shard_map/ppermute | solution.py:24
  31.6 7.9 %collective-permute-start.7 = (bf16[128,128]{1,0:T(8,128)(2,1)S(1)}, bf16[128,128]{1,0:T(8,128)(2,1)S(1)}, u32[]{:S(2)}, u32[]{:S(2)}) collective-permute-start(bf16[128,128]{1,0:T(8,128)(2,1)S(1)} %fusion.5.refs_0_), channel_id=1, source_target_pairs={{0,2},{1,3},{2,0},{3,1},{4,6},{5,7},{6,4},{7,5},{8,10},{9,11},{10,... | collective-permute-start | bytes 98312 | tf_op jit(solution)/shard_map/ppermute | solution.py:24
  31.7 7.8 %collective-permute-start.8 = (bf16[128,128]{1,0:T(8,128)(2,1)S(1)}, bf16[128,128]{1,0:T(8,128)(2,1)S(1)}, u32[]{:S(2)}, u32[]{:S(2)}) collective-permute-start(bf16[128,128]{1,0:T(8,128)(2,1)S(1)} %fusion.5.refs_0_), channel_id=1, source_target_pairs={{0,4},{1,5},{2,6},{3,7},{4,0},{5,1},{6,2},{7,3},{8,12},{9,13},{10,... | collective-permute-start | bytes 98312 | tf_op jit(solution)/shard_map/ppermute | solution.py:24
  50.1 7.7 %collective-permute-start.14 = (bf16[128,128]{1,0:T(8,128)(2,1)S(1)}, bf16[128,128]{1,0:T(8,128)(2,1)S(1)}, u32[]{:S(2)}, u32[]{:S(2)}) collective-permute-start(bf16[128,128]{1,0:T(8,128)(2,1)S(1)} %fusion.4.refs_0_), channel_id=1, source_target_pairs={{0,2},{1,3},{2,0},{3,1},{4,6},{5,7},{6,4},{7,5},{8,10},{9,11},{10,... | collective-permute-start | bytes 98312 | tf_op jit(solution)/shard_map/ppermute | solution.py:24
  50.2 7.7 %collective-permute-start.15 = (bf16[128,128]{1,0:T(8,128)(2,1)S(1)}, bf16[128,128]{1,0:T(8,128)(2,1)S(1)}, u32[]{:S(2)}, u32[]{:S(2)}) collective-permute-start(bf16[128,128]{1,0:T(8,128)(2,1)S(1)} %fusion.4.refs_0_), channel_id=1, source_target_pairs={{0,4},{1,5},{2,6},{3,7},{4,0},{5,1},{6,2},{7,3},{8,12},{9,13},{10,... | collective-permute-start | bytes 98312 | tf_op jit(solution)/shard_map/ppermute | solution.py:24
  65.9 7.6 %collective-permute-start.20 = (bf16[128,128]{1,0:T(8,128)(2,1)S(1)}, bf16[128,128]{1,0:T(8,128)(2,1)S(1)}, u32[]{:S(2)}, u32[]{:S(2)}) collective-permute-start(bf16[128,128]{1,0:T(8,128)(2,1)S(1)} %fusion.3.refs_0_), channel_id=1, source_target_pairs={{0,2},{1,3},{2,0},{3,1},{4,6},{5,7},{6,4},{7,5},{8,10},{9,11},{10,... | collective-permute-start | bytes 98312 | tf_op jit(solution)/shard_map/ppermute | solution.py:24
  66.0 7.6 %collective-permute-start.21 = (bf16[128,128]{1,0:T(8,128)(2,1)S(1)}, bf16[128,128]{1,0:T(8,128)(2,1)S(1)}, u32[]{:S(2)}, u32[]{:S(2)}) collective-permute-start(bf16[128,128]{1,0:T(8,128)(2,1)S(1)} %fusion.3.refs_0_), channel_id=1, source_target_pairs={{0,4},{1,5},{2,6},{3,7},{4,0},{5,1},{6,2},{7,3},{8,12},{9,13},{10,... | collective-permute-start | bytes 98312 | tf_op jit(solution)/shard_map/ppermute | solution.py:24
  76.8 10.4 %collective-permute-start.25 = (bf16[128,128]{1,0:T(8,128)(2,1)S(1)}, bf16[128,128]{1,0:T(8,128)(2,1)S(1)}, u32[]{:S(2)}, u32[]{:S(2)}) collective-permute-start(bf16[128,128]{1,0:T(8,128)(2,1)S(1)} %get-tuple-element.115), channel_id=1, source_target_pairs={{0,24},{8,16},{16,8},{24,0},{1,25},{9,17},{17,9},{25,1},{2,26},{10... | collective-permute-start | bytes 98312 | tf_op jit(solution)/shard_map/ppermute | solution.py:24
  79.3 7.9 %collective-permute-start.24 = (bf16[128,128]{1,0:T(8,128)(2,1)S(1)}, bf16[128,128]{1,0:T(8,128)(2,1)S(1)}, u32[]{:S(2)}, u32[]{:S(2)}) collective-permute-start(bf16[128,128]{1,0:T(8,128)(2,1)S(1)} %get-tuple-element.114), channel_id=1, source_target_pairs={{0,16},{8,24},{16,0},{24,8},{1,17},{9,25},{17,1},{25,9},{2,18},{10... | collective-permute-start | bytes 98312 | tf_op jit(solution)/shard_map/ppermute | solution.py:24
  79.8 9.0 %collective-permute-start.23 = (bf16[128,128]{1,0:T(8,128)(2,1)S(1)}, bf16[128,128]{1,0:T(8,128)(2,1)S(1)}, u32[]{:S(2)}, u32[]{:S(2)}) collective-permute-start(bf16[128,128]{1,0:T(8,128)(2,1)S(1)} %get-tuple-element.113), channel_id=1, source_target_pairs={{0,8},{8,0},{16,24},{24,16},{1,9},{9,1},{17,25},{25,17},{2,10},{10... | collective-permute-start | bytes 98312 | tf_op jit(solution)/shard_map/ppermute | solution.py:24
  80.4 10.8 %collective-permute-start.44 = (bf16[2,64,512]{2,1,0:T(8,128)(2,1)S(1)}, bf16[2,64,512]{2,1,0:T(8,128)(2,1)S(1)}, u32[]{:S(2)}, u32[]{:S(2)}) collective-permute-start(bf16[2,64,512]{2,1,0:T(8,128)(2,1)S(1)} %get-tuple-element.202), channel_id=1, source_target_pairs={{0,4},{1,5},{2,6},{3,7},{4,0},{5,1},{6,2},{7,3},{8,12},{9,13},{10,... | collective-permute-start | bytes 393224 | tf_op jit(solution)/shard_map/ppermute | solution.py:24
  85.0 14.7 %collective-permute-start.46 = (bf16[2,64,512]{2,1,0:T(8,128)(2,1)S(1)}, bf16[2,64,512]{2,1,0:T(8,128)(2,1)S(1)}, u32[]{:S(2)}, u32[]{:S(2)}) collective-permute-start(bf16[2,64,512]{2,1,0:T(8,128)(2,1)S(1)} %get-tuple-element.202), channel_id=1, source_target_pairs={{0,6},{1,7},{2,4},{3,5},{4,2},{5,3},{6,0},{7,1},{8,14},{9,15},{10,... | collective-permute-start | bytes 393224 | tf_op jit(solution)/shard_map/ppermute | solution.py:24
  87.2 11.1 %collective-permute-start.43 = (bf16[2,64,512]{2,1,0:T(8,128)(2,1)S(1)}, bf16[2,64,512]{2,1,0:T(8,128)(2,1)S(1)}, u32[]{:S(2)}, u32[]{:S(2)}) collective-permute-start(bf16[2,64,512]{2,1,0:T(8,128)(2,1)S(1)} %get-tuple-element.201), channel_id=1, source_target_pairs={{0,4},{1,5},{2,6},{3,7},{4,0},{5,1},{6,2},{7,3},{8,12},{9,13},{10,... | collective-permute-start | bytes 393224 | tf_op jit(solution)/shard_map/ppermute | solution.py:24
  87.2 13.6 %collective-permute-start.45 = (bf16[2,64,512]{2,1,0:T(8,128)(2,1)S(1)}, bf16[2,64,512]{2,1,0:T(8,128)(2,1)S(1)}, u32[]{:S(2)}, u32[]{:S(2)}) collective-permute-start(bf16[2,64,512]{2,1,0:T(8,128)(2,1)S(1)} %get-tuple-element.201), channel_id=1, source_target_pairs={{0,6},{1,7},{2,4},{3,5},{4,2},{5,3},{6,0},{7,1},{8,14},{9,15},{10,... | collective-permute-start | bytes 393224 | tf_op jit(solution)/shard_map/ppermute | solution.py:24
  88.9 12.0 %collective-permute-start.26 = (bf16[128,128]{1,0:T(8,128)(2,1)S(1)}, bf16[128,128]{1,0:T(8,128)(2,1)S(1)}, u32[]{:S(2)}, u32[]{:S(2)}) collective-permute-start(bf16[128,128]{1,0:T(8,128)(2,1)S(1)} %fusion.2.refs_0_), channel_id=1, source_target_pairs={{0,2},{1,3},{2,0},{3,1},{4,6},{5,7},{6,4},{7,5},{8,10},{9,11},{10,... | collective-permute-start | bytes 98312 | tf_op jit(solution)/shard_map/ppermute | solution.py:24
  91.2 22.3 %collective-permute-start.39 = (bf16[4,64,512]{2,1,0:T(8,128)(2,1)S(1)}, bf16[4,64,512]{2,1,0:T(8,128)(2,1)S(1)}, u32[]{:S(2)}, u32[]{:S(2)}) collective-permute-start(bf16[4,64,512]{2,1,0:T(8,128)(2,1)S(1)} %copy-done.5), channel_id=1, source_target_pairs={{0,8},{8,0},{16,24},{24,16},{1,9},{9,1},{17,25},{25,17},{2,10},{10... | collective-permute-start | bytes 786440 | tf_op jit(solution)/shard_map/ppermute | solution.py:24
  98.3 15.2 %collective-permute-start.40 = (bf16[4,64,512]{2,1,0:T(8,128)(2,1)S(1)}, bf16[4,64,512]{2,1,0:T(8,128)(2,1)S(1)}, u32[]{:S(2)}, u32[]{:S(2)}) collective-permute-start(bf16[4,64,512]{2,1,0:T(8,128)(2,1)S(1)} %copy-done.5), channel_id=1, source_target_pairs={{0,16},{8,24},{16,0},{24,8},{1,17},{9,25},{17,1},{25,9},{2,18},{10... | collective-permute-start | bytes 786440 | tf_op jit(solution)/shard_map/ppermute | solution.py:24
  99.7 13.8 %collective-permute-start.41 = (bf16[4,64,512]{2,1,0:T(8,128)(2,1)S(1)}, bf16[4,64,512]{2,1,0:T(8,128)(2,1)S(1)}, u32[]{:S(2)}, u32[]{:S(2)}) collective-permute-start(bf16[4,64,512]{2,1,0:T(8,128)(2,1)S(1)} %copy-done.5), channel_id=1, source_target_pairs={{0,24},{8,16},{16,8},{24,0},{1,25},{9,17},{17,9},{25,1},{2,26},{10... | collective-permute-start | bytes 786440 | tf_op jit(solution)/shard_map/ppermute | solution.py:24
  100.8 12.6 %collective-permute-start.42 = (bf16[4,64,512]{2,1,0:T(8,128)(2,1)S(1)}, bf16[4,64,512]{2,1,0:T(8,128)(2,1)S(1)}, u32[]{:S(2)}, u32[]{:S(2)}) collective-permute-start(bf16[4,64,512]{2,1,0:T(8,128)(2,1)S(1)} %get-tuple-element.140.refs_4_), channel_id=1, source_target_pairs={{0,2},{1,3},{2,0},{3,1},{4,6},{5,7},{6,4},{7,5},{8,10},{9,11},{10,... | collective-permute-start | bytes 786440 | tf_op jit(solution)/shard_map/ppermute | solution.py:24
  113.6 16.6 %collective-permute-start.47 = (bf16[4,4,64,512]{3,2,1,0:T(8,128)(2,1)S(1)}, bf16[4,4,64,512]{3,2,1,0:T(8,128)(2,1)S(1)}, u32[]{:S(2)}, u32[]{:S(2)}) collective-permute-start(bf16[4,4,64,512]{3,2,1,0:T(8,128)(2,1)S(1)} %pad_maximum_fusion), channel_id=1, source_target_pairs={{0,1},{1,0},{2,3},{3,2},{4,5},{5,4},{6,7},{7,6},{8,9},{9,8},{10,11... | collective-permute-start | bytes 3145736 | tf_op jit(solution)/shard_map/ppermute | solution.py:24
  118.8 32.7 %collective-permute-start.55 = (bf16[16,64,512]{2,1,0:T(8,128)(2,1)S(1)}, bf16[16,64,512]{2,1,0:T(8,128)(2,1)S(1)}, u32[]{:S(2)}, u32[]{:S(2)}) collective-permute-start(bf16[16,64,512]{2,1,0:T(8,128)(2,1)S(1)} %shard_map.78.refs_9_.refs_6_), channel_id=1, source_target_pairs={{0,1},{1,0},{2,3},{3,2},{4,5},{5,4},{6,7},{7,6},{8,9},{9,8},{10,11... | collective-permute-start | bytes 3145736 | tf_op jit(solution)/shard_map/ppermute | solution.py:24
  131.6 7.8 %collective-permute-start.48 = (bf16[4,64,512]{2,1,0:T(8,128)(2,1)S(1)}, bf16[4,64,512]{2,1,0:T(8,128)(2,1)S(1)}, u32[]{:S(2)}, u32[]{:S(2)}) collective-permute-start(bf16[4,64,512]{2,1,0:T(8,128)(2,1)S(1)} %shard_map.79.refs_6_), channel_id=1, source_target_pairs={{0,1},{1,0},{2,3},{3,2},{4,5},{5,4},{6,7},{7,6},{8,9},{9,8},{10,11... | collective-permute-start | bytes 786440 | tf_op jit(solution)/shard_map/ppermute | solution.py:24
  136.3 26.9 %collective-permute-start.62 = (bf16[4,64,512]{2,1,0:T(8,128)(2,1)S(1)}, bf16[4,64,512]{2,1,0:T(8,128)(2,1)S(1)}, u32[]{:S(2)}, u32[]{:S(2)}) collective-permute-start(bf16[4,64,512]{2,1,0:T(8,128)(2,1)S(1)} %copy-done.3), channel_id=1, source_target_pairs={{0,8},{8,0},{16,24},{24,16},{1,9},{9,1},{17,25},{25,17},{2,10},{10... | collective-permute-start | bytes 786440 | tf_op jit(solution)/shard_map/ppermute | solution.py:24
  147.8 15.4 %collective-permute-start.63 = (bf16[2,64,512]{2,1,0:T(8,128)(2,1)S(1)}, bf16[2,64,512]{2,1,0:T(8,128)(2,1)S(1)}, u32[]{:S(2)}, u32[]{:S(2)}) collective-permute-start(bf16[2,64,512]{2,1,0:T(8,128)(2,1)S(1)} %get-tuple-element.159.refs_2_), channel_id=1, source_target_pairs={{0,2},{1,3},{2,0},{3,1},{4,6},{5,7},{6,4},{7,5},{8,10},{9,11},{10,... | collective-permute-start | bytes 393224 | tf_op jit(solution)/shard_map/ppermute | solution.py:24
  151.6 11.6 %collective-permute-start.64 = (bf16[2,64,512]{2,1,0:T(8,128)(2,1)S(1)}, bf16[2,64,512]{2,1,0:T(8,128)(2,1)S(1)}, u32[]{:S(2)}, u32[]{:S(2)}) collective-permute-start(bf16[2,64,512]{2,1,0:T(8,128)(2,1)S(1)} %get-tuple-element.159.refs_2_), channel_id=1, source_target_pairs={{0,4},{1,5},{2,6},{3,7},{4,0},{5,1},{6,2},{7,3},{8,12},{9,13},{10,... | collective-permute-start | bytes 393224 | tf_op jit(solution)/shard_map/ppermute | solution.py:24
  154.2 9.0 %collective-permute-start.65 = (bf16[2,64,512]{2,1,0:T(8,128)(2,1)S(1)}, bf16[2,64,512]{2,1,0:T(8,128)(2,1)S(1)}, u32[]{:S(2)}, u32[]{:S(2)}) collective-permute-start(bf16[2,64,512]{2,1,0:T(8,128)(2,1)S(1)} %get-tuple-element.159.refs_2_), channel_id=1, source_target_pairs={{0,6},{1,7},{2,4},{3,5},{4,2},{5,3},{6,0},{7,1},{8,14},{9,15},{10,... | collective-permute-start | bytes 393224 | tf_op jit(solution)/shard_map/ppermute | solution.py:24
  163.3 8.4 %collective-permute-start.66 = (bf16[4,2,64,512]{3,2,1,0:T(8,128)(2,1)S(1)}, bf16[4,2,64,512]{3,2,1,0:T(8,128)(2,1)S(1)}, u32[]{:S(2)}, u32[]{:S(2)}) collective-permute-start(bf16[4,2,64,512]{3,2,1,0:T(8,128)(2,1)S(1)} %pad_maximum_fusion.1), channel_id=1, source_target_pairs={{0,1},{1,0},{2,3},{3,2},{4,5},{5,4},{6,7},{7,6},{8,9},{9,8},{10,11... | collective-permute-start | bytes 1572872 | tf_op jit(solution)/shard_map/ppermute | solution.py:24
  163.9 8.9 %collective-permute-start.58 = (bf16[2,128,128]{2,1,0:T(8,128)(2,1)S(1)}, bf16[2,128,128]{2,1,0:T(8,128)(2,1)S(1)}, u32[]{:S(2)}, u32[]{:S(2)}) collective-permute-start(bf16[2,128,128]{2,1,0:T(8,128)(2,1)S(1)} %get-tuple-element.153), channel_id=1, source_target_pairs={{0,6},{1,7},{2,4},{3,5},{4,2},{5,3},{6,0},{7,1},{8,14},{9,15},{10,... | collective-permute-start | bytes 196616 | tf_op jit(solution)/shard_map/ppermute | solution.py:24
  166.1 7.1 %collective-permute-start.57 = (bf16[2,128,128]{2,1,0:T(8,128)(2,1)S(1)}, bf16[2,128,128]{2,1,0:T(8,128)(2,1)S(1)}, u32[]{:S(2)}, u32[]{:S(2)}) collective-permute-start(bf16[2,128,128]{2,1,0:T(8,128)(2,1)S(1)} %get-tuple-element.152), channel_id=1, source_target_pairs={{0,4},{1,5},{2,6},{3,7},{4,0},{5,1},{6,2},{7,3},{8,12},{9,13},{10,... | collective-permute-start | bytes 196616 | tf_op jit(solution)/shard_map/ppermute | solution.py:24
  172.8 7.3 %collective-permute-start.67 = (bf16[4,64,512]{2,1,0:T(8,128)(2,1)S(1)}, bf16[4,64,512]{2,1,0:T(8,128)(2,1)S(1)}, u32[]{:S(2)}, u32[]{:S(2)}) collective-permute-start(bf16[4,64,512]{2,1,0:T(8,128)(2,1)S(1)} %shard_map.83.refs_6_), channel_id=1, source_target_pairs={{0,1},{1,0},{2,3},{3,2},{4,5},{5,4},{6,7},{7,6},{8,9},{9,8},{10,11... | collective-permute-start | bytes 786440 | tf_op jit(solution)/shard_map/ppermute | solution.py:24
  (49 other events, 277.3 us)
